TPU v7x, 256 devices: a whole 4x4x8 slice. The times are simulated.
256 devices in a mesh: layer: 4 (over z_hi, core), doc: 64 (over y, x, z_lo).
Axes of the slice: x: 4, y: 4, z: 8 (z_hi: 2, z_lo: 4; z = z_hi * 4 + z_lo), core: 2. Of those that a mesh axis runs over, the one named last changes fastest.
Arguments:
- query_grads: bfloat16 [4, 256, 4096], P('layer', 'doc'), may hold values from -6 to 6
- stored_grads: bfloat16 [4, 65536, 4096], P('layer', 'doc'), may hold values from -0.0234375 to 0.0234375
- basis_in: float32 [4, 64, 64], P('layer'), may hold values from -0.75 to 0.75
- basis_out: float32 [4, 64, 64], P('layer'), may hold values from -0.75 to 0.75
- eigen_values: float32 [4, 64, 64], P('layer'), may hold values from 0.02 to 4
- layer_mask: int32 [256, 4], P(None, 'layer'), may hold values 0 or 1
- doc_counts: int32 [64], P('doc'), may hold values from 1 to 1024, 32768 in all
Outputs:
- scores: float32 [256, 65536], P('layer', 'doc')
Inputs may be any that keep to these rules, and one draw needn't show every extreme that they name: `doc_counts`: the counts sum to 32768 and the largest equals 1024.
All inputs are finite; a program needn't handle non-finite values. No bound on the sum of `layer_mask` or of `doc_counts` on one device may be relied on, other than what follows from the above.
Results may differ from a plain program's by a relative error of at most 0.0029.
Values may be sent and summed in bfloat16 or wider, within the bound.
No kernel may reach another device: no remote copies, remote signals or barrier semaphores. Data moves between devices by JAX's collectives and lax.ppermute only.
A program may use at most 64 MiB of HBM per device.

v0:
```python
import functools

import jax
import jax.numpy as jnp
from jax import lax
from jax.experimental import pallas as pl
from jax.experimental.pallas import tpu as pltpu
from jax.sharding import PartitionSpec as P

damping = 0.1

side = 4


def doc_pairs(stride, flip):
    return [(d, d ^ (flip * stride)) for d in range(side**3)]


def layer_pairs(flip):
    return [(l, l ^ flip) for l in range(4)]


def exact_dot(a, b, dims):
    return lax.dot_general(
        a, b, (dims, ((), ())), precision=lax.Precision.HIGHEST, preferred_element_type=jnp.float32
    )


def precondition_kernel(mask_ref, doc_ref, grads_ref, basis_in_ref, basis_out_ref, eigen_ref, out_ref):
    count, out_size, in_size = grads_ref.shape[0], basis_out_ref.shape[0], basis_in_ref.shape[0]
    base_in, base_out = basis_in_ref[...], basis_out_ref[...]
    divisor = eigen_ref[...] + damping
    grads = grads_ref[...].astype(jnp.float32).reshape(count, out_size, in_size)
    blocks = [grads[q] for q in range(count)]
    side_by_side = exact_dot(base_out, jnp.concatenate(blocks, axis=1), ((0,), (0,)))
    stacked = jnp.concatenate(jnp.split(side_by_side, count, axis=1), axis=0)
    rotated = exact_dot(stacked, base_in, ((1,), (0,)))
    scaled = rotated / jnp.concatenate([divisor] * count, axis=0)
    half = exact_dot(scaled, base_in, ((1,), (1,)))
    side_by_side = jnp.concatenate(jnp.split(half, count, axis=0), axis=1)
    restored = exact_dot(base_out, side_by_side, ((1,), (0,)))
    rows = []
    for q, block in enumerate(jnp.split(restored, count, axis=1)):
        weight = mask_ref[doc_ref[0] * count + q].astype(jnp.float32)
        rows.append(block * weight)
    out_ref[...] = jnp.stack(rows).reshape(count, out_size * in_size).astype(jnp.bfloat16)


def precondition(gradients, basis_in, basis_out, eigen_values, mask, doc):
    vmem, smem = pl.BlockSpec(memory_space=pltpu.VMEM), pl.BlockSpec(memory_space=pltpu.SMEM)
    operands = [
        pltpu.with_memory_space_constraint(a, pltpu.HBM)
        for a in (mask, gradients, basis_in, basis_out, eigen_values)
    ]
    return pl.pallas_call(
        precondition_kernel,
        out_shape=jax.ShapeDtypeStruct(gradients.shape, jnp.bfloat16),
        in_specs=[smem, smem, vmem, vmem, vmem, vmem],
        out_specs=vmem,
        compiler_params=pltpu.CompilerParams(vmem_limit_bytes=4 << 20),
        name="precondition",
    )(operands[0], doc.reshape(1), *operands[1:])


straight = (
    [(0, 0, h) for h in range(2)]
    + [(0, k, h) for k in (1, 2, 3) for h in range(2)]
    + [(k, 0, h) for k in (1, 2, 3) for h in range(2)]
)
diagonal = [(j, i, 0) for i in (1, 2, 3) for j in (1, 2, 3)] + [
    (j, i, 1) for j in (1, 2, 3) for i in (1, 2, 3)
]


def place_kernel(tiles, place_ref, *refs):
    out_ref = refs[-1]
    core_row, far_row, x = place_ref[0], place_ref[1], place_ref[2]
    t = 0
    for piece in refs:
        if t == len(tiles):
            break
        for row in range(0, piece.shape[0], 8):
            ky, kx, half = tiles[t]
            out_ref[core_row ^ (ky & 1), far_row ^ (ky >> 1), x ^ kx, half] = piece[row : row + 8]
            t += 1


def placed(tiles, place, pieces, flops, begun=None):
    vmem, smem = pl.BlockSpec(memory_space=pltpu.VMEM), pl.BlockSpec(memory_space=pltpu.SMEM)
    width = pieces[0].shape[1]
    operands = pieces + ([] if begun is None else [begun])
    return pl.pallas_call(
        functools.partial(place_kernel, tiles),
        out_shape=jax.ShapeDtypeStruct((2, 2, 4, 2, 8, width), jnp.bfloat16),
        in_specs=[smem] + [vmem] * len(operands),
        out_specs=vmem,
        input_output_aliases={} if begun is None else {len(operands): 0},
        compiler_params=pltpu.CompilerParams(vmem_limit_bytes=8 << 20),
        cost_estimate=pl.CostEstimate(flops=flops, bytes_accessed=0, transcendentals=0),
        name="placed",
    )(place, *operands)


def score_kernel(queries_ref, stored_ref, out_ref):
    width = 256

    def tile(i, carry):
        columns = pl.ds(pl.multiple_of(i * width, width), width)
        out_ref[:, columns] = lax.dot_general(
            queries_ref[...],
            stored_ref[columns, :],
            (((1,), (1,)), ((), ())),
            preferred_element_type=jnp.float32,
        )
        return carry

    lax.fori_loop(0, stored_ref.shape[0] // width, tile, 0)


def score(queries, stored):
    vmem = pl.BlockSpec(memory_space=pltpu.VMEM)
    rows, slots = queries.shape[0], stored.shape[0]
    return pl.pallas_call(
        score_kernel,
        out_shape=jax.ShapeDtypeStruct((rows, slots), jnp.float32),
        in_specs=[vmem, vmem],
        out_specs=vmem,
        compiler_params=pltpu.CompilerParams(vmem_limit_bytes=8 << 20),
        cost_estimate=pl.CostEstimate(
            flops=2 * queries.size * slots, bytes_accessed=0, transcendentals=0
        ),
        name="score",
    )(queries, stored)


def fetch(block, stride):
    blocks = []
    for k in (1, 2, 3):
        blocks.append(lax.ppermute(block, "doc", doc_pairs(stride, k)))
    return blocks


def ordered(blocks, coordinate):
    low, high = (coordinate & 1) == 1, (coordinate & 2) == 2
    a, b, c, d = blocks
    a, b, c, d = (jnp.where(low, p, q) for p, q in ((b, a), (a, b), (d, c), (c, d)))
    return [jnp.where(high, p, q) for p, q in ((c, a), (d, b), (a, c), (b, d))]


def on_device(query_grads, stored_grads, basis_in, basis_out, eigen_values, layer_mask, doc_counts):
    doc, layer = lax.axis_index("doc"), lax.axis_index("layer")
    y, x, z = doc // 16, (doc // 4) % 4, doc % 4
    stored = pltpu.with_memory_space_constraint(stored_grads[0], pltpu.VMEM)
    own = precondition(
        query_grads[0], basis_in[0], basis_out[0], eigen_values[0], layer_mask[:, 0], doc
    )

    rows = ordered([own] + fetch(own, 1), z)
    block = lax.optimization_barrier(jnp.concatenate(rows, axis=0))
    along_y, along_x = fetch(block, 16), fetch(block, 4)
    core, far = layer & 1, layer >> 1
    place = jnp.stack([(y & 1) ^ core, (y >> 1) ^ far, x]).astype(jnp.int32)
    queries = placed(straight, place, [block] + along_x + along_y, 2 * 10**10)
    upper = jnp.concatenate([b[:8] for b in along_y])
    lower = jnp.concatenate([b[8:] for b in along_x])
    diagonals = fetch(upper, 4) + fetch(lower, 16)
    queries = placed(diagonal, place, diagonals, 10**8, queries)
    tiles = score(queries.reshape(256, -1), stored)
    tiles = tiles.reshape(2, 2, 4, 2, 8, -1)
    other = lax.ppermute(tiles[1], "layer", layer_pairs(1))
    give = (tiles[0, 1] + other[1]).astype(jnp.bfloat16)
    other_far = lax.ppermute(give, "layer", layer_pairs(2))
    total = tiles[0, 0] + other[0] + other_far.astype(jnp.float32)
    slots = stored.shape[0]
    total = total.reshape(64, slots)
    live_slots = jnp.arange(slots, dtype=jnp.int32) < doc_counts[0]
    return jnp.where(live_slots[None, :], total, jnp.zeros_like(total))


def solution(mesh):
    in_specs = (
        P("layer", "doc", None),
        P("layer", "doc", None),
        P("layer", None, None),
        P("layer", None, None),
        P("layer", None, None),
        P(None, "layer"),
        P("doc"),
    )
    out_specs = P("layer", "doc")
    return jax.shard_map(
        on_device, mesh=mesh, in_specs=in_specs, out_specs=out_specs, check_vma=False
    )
```

profile of v0, /device:TPU:64, one launch (start us, length us, event | category | flops | bytes accessed | tf_op | source)
XLA Modules:
  0.0 58.9 jit_solution(2369200385488123419)
XLA Ops:
  0.0 2.3 %precondition.1 = bf16[4,4096]{1,0:T(4,128)(2,1)S(1)} custom-call(s32[256]{0:T(256)} %bitcast.48, s32[1]{0:T(128)} %bitcast.5.doc_ref, bf16[4,4096]{1,0:T(4,128)(2,1)} %bitcast.44, f32[64,64]{1,0:T(8,128)} %bitcast.45, f32[64,64]{1,0:T(8,128)} %bitcast.46, f32[64,64]{1,0:T(8,128)} %bitcast.47), custom_call_target="tpu_custom_call" | custom-call | tf_op jit(solution)/shard_map/precondition/pallas_call | solution.py:55
  2.5 4.2 %collective-permute-start.1 = (bf16[4,4096]{1,0:T(4,128)(2,1)S(1)}, bf16[4,4096]{1,0:T(4,128)(2,1)S(1)}, u32[]{:S(2)}, u32[]{:S(2)}) collective-permute-start(bf16[4,4096]{1,0:T(4,128)(2,1)S(1)} %precondition.1), channel_id=1, source_target_pairs={{0,2},{1,3},{2,0},{3,1},{4,6},{5,7},{6,4},{7,5},{8,10},{9,11},{10,... | collective-permute-start | bytes 98312 | tf_op jit(solution)/shard_map/ppermute | solution.py:139
  6.7 2.3 %collective-permute-done.1 = bf16[4,4096]{1,0:T(4,128)(2,1)S(1)} collective-permute-done((bf16[4,4096]{1,0:T(4,128)(2,1)S(1)}, bf16[4,4096]{1,0:T(4,128)(2,1)S(1)}, u32[]{:S(2)}, u32[]{:S(2)}) %collective-permute-start.1) | collective-permute-done | bytes 32800 | tf_op jit(solution)/shard_map/ppermute | solution.py:139
  9.0 1.6 %collective-permute-done.2 = bf16[4,4096]{1,0:T(4,128)(2,1)S(1)} collective-permute-done((bf16[4,4096]{1,0:T(4,128)(2,1)S(1)}, bf16[4,4096]{1,0:T(4,128)(2,1)S(1)}, u32[]{:S(2)}, u32[]{:S(2)}) %collective-permute-start.2) | collective-permute-done | bytes 32800 | tf_op jit(solution)/shard_map/ppermute | solution.py:139
  10.8 1.6 %collective-permute-start.9 = (bf16[16,4096]{1,0:T(8,128)(2,1)S(1)}, bf16[16,4096]{1,0:T(8,128)(2,1)S(1)}, u32[]{:S(2)}, u32[]{:S(2)}) collective-permute-start(bf16[16,4096]{1,0:T(8,128)(2,1)S(1)} %pad_maximum_fusion.2.refs_0_), channel_id=1, source_target_pairs={{0,4},{1,5},{2,6},{3,7},{4,0},{5,1},{6,2},{7,3},{8,12},{9,13},{10,... | collective-permute-start | bytes 393224 | tf_op jit(solution)/shard_map/ppermute | solution.py:139
  12.4 2.7 %collective-permute-start.10 = (bf16[16,4096]{1,0:T(8,128)(2,1)S(1)}, bf16[16,4096]{1,0:T(8,128)(2,1)S(1)}, u32[]{:S(2)}, u32[]{:S(2)}) collective-permute-start(bf16[16,4096]{1,0:T(8,128)(2,1)S(1)} %pad_maximum_fusion.2.refs_0_), channel_id=1, source_target_pairs={{0,8},{1,9},{2,10},{3,11},{4,12},{5,13},{6,14},{7,15},{8,0},{9,1},... | collective-permute-start | bytes 393224 | tf_op jit(solution)/shard_map/ppermute | solution.py:139
  15.1 0.5 collective-permute-start.11
  15.6 1.6 %collective-permute-start.3 = (bf16[16,4096]{1,0:T(8,128)(2,1)S(1)}, bf16[16,4096]{1,0:T(8,128)(2,1)S(1)}, u32[]{:S(2)}, u32[]{:S(2)}) collective-permute-start(bf16[16,4096]{1,0:T(8,128)(2,1)S(1)} %pad_maximum_fusion.2.refs_0_), channel_id=1, source_target_pairs={{0,16},{1,17},{2,18},{3,19},{4,20},{5,21},{6,22},{7,23},{8,24},{9,... | collective-permute-start | bytes 393224 | tf_op jit(solution)/shard_map/ppermute | solution.py:139
  17.2 2.9 %collective-permute-start.4 = (bf16[16,4096]{1,0:T(8,128)(2,1)S(1)}, bf16[16,4096]{1,0:T(8,128)(2,1)S(1)}, u32[]{:S(2)}, u32[]{:S(2)}) collective-permute-start(bf16[16,4096]{1,0:T(8,128)(2,1)S(1)} %pad_maximum_fusion.2.refs_0_), channel_id=1, source_target_pairs={{0,32},{1,33},{2,34},{3,35},{4,36},{5,37},{6,38},{7,39},{8,40},{9,... | collective-permute-start | bytes 393224 | tf_op jit(solution)/shard_map/ppermute | solution.py:139
  20.4 0.9 %collective-permute-done.11.refs_3_ = bf16[16,4096]{1,0:T(8,128)(2,1)S(1)} collective-permute-done((bf16[16,4096]{1,0:T(8,128)(2,1)S(1)}, bf16[16,4096]{1,0:T(8,128)(2,1)S(1)}, u32[]{:S(2)}, u32[]{:S(2)}) %collective-permute-start.11) | collective-permute-done | bytes 131104 | tf_op jit(solution)/shard_map/ppermute | solution.py:139
  21.3 1.7 %collective-permute-start.12 = (bf16[24,4096]{1,0:T(8,128)(2,1)S(1)}, bf16[24,4096]{1,0:T(8,128)(2,1)S(1)}, u32[]{:S(2)}, u32[]{:S(2)}) collective-permute-start(bf16[24,4096]{1,0:T(8,128)(2,1)S(1)} %pad_maximum_fusion.1), channel_id=1, source_target_pairs={{0,16},{1,17},{2,18},{3,19},{4,20},{5,21},{6,22},{7,23},{8,24},{9,... | collective-permute-start | bytes 589832 | tf_op jit(solution)/shard_map/ppermute | solution.py:139
  23.0 2.9 %collective-permute-start.13 = (bf16[24,4096]{1,0:T(8,128)(2,1)S(1)}, bf16[24,4096]{1,0:T(8,128)(2,1)S(1)}, u32[]{:S(2)}, u32[]{:S(2)}) collective-permute-start(bf16[24,4096]{1,0:T(8,128)(2,1)S(1)} %pad_maximum_fusion.1), channel_id=1, source_target_pairs={{0,32},{1,33},{2,34},{3,35},{4,36},{5,37},{6,38},{7,39},{8,40},{9,... | collective-permute-start | bytes 589832 | tf_op jit(solution)/shard_map/ppermute | solution.py:139
  26.1 1.6 %collective-permute-done.5.refs_6_ = bf16[16,4096]{1,0:T(8,128)(2,1)S(1)} collective-permute-done((bf16[16,4096]{1,0:T(8,128)(2,1)S(1)}, bf16[16,4096]{1,0:T(8,128)(2,1)S(1)}, u32[]{:S(2)}, u32[]{:S(2)}) %collective-permute-start.5) | collective-permute-done | bytes 131104 | tf_op jit(solution)/shard_map/ppermute | solution.py:139
  27.7 0.7 %collective-permute-start.6 = (bf16[24,4096]{1,0:T(8,128)(2,1)S(1)}, bf16[24,4096]{1,0:T(8,128)(2,1)S(1)}, u32[]{:S(2)}, u32[]{:S(2)}) collective-permute-start(bf16[24,4096]{1,0:T(8,128)(2,1)S(1)} %pad_maximum_fusion), channel_id=1, source_target_pairs={{0,4},{1,5},{2,6},{3,7},{4,0},{5,1},{6,2},{7,3},{8,12},{9,13},{10,... | collective-permute-start | bytes 589832 | tf_op jit(solution)/shard_map/ppermute | solution.py:139
  28.4 6.5 %collective-permute-start.7 = (bf16[24,4096]{1,0:T(8,128)(2,1)S(1)}, bf16[24,4096]{1,0:T(8,128)(2,1)S(1)}, u32[]{:S(2)}, u32[]{:S(2)}) collective-permute-start(bf16[24,4096]{1,0:T(8,128)(2,1)S(1)} %pad_maximum_fusion), channel_id=1, source_target_pairs={{0,8},{1,9},{2,10},{3,11},{4,12},{5,13},{6,14},{7,15},{8,0},{9,1},... | collective-permute-start | bytes 589832 | tf_op jit(solution)/shard_map/ppermute | solution.py:139
  35.0 0.6 %placed.2.refs_6_ = bf16[2,2,4,2,8,4096]{5,4,3,2,1,0:T(8,128)(2,1)S(1)} custom-call(s32[3]{0:T(128)S(1)} %pad_add_fusion.place_ref, bf16[16,4096]{1,0:T(8,128)(2,1)S(1)} %pad_maximum_fusion.2.refs_0_, bf16[16,4096]{1,0:T(8,128)(2,1)S(1)} %collective-permute-done.9.refs_1_, bf16[16,4096]{1,0:T(8,128)(2,1)S(1)} %collective-permute-done.10.refs_2_, ...), custom_call_target="tpu_custom_call" | custom-call | flops 20000000000 | tf_op jit(solution)/shard_map/placed/pallas_call | solution.py:92
  35.6 5.2 %collective-permute-done.7.refs_1_ = bf16[24,4096]{1,0:T(8,128)(2,1)S(1)} collective-permute-done((bf16[24,4096]{1,0:T(8,128)(2,1)S(1)}, bf16[24,4096]{1,0:T(8,128)(2,1)S(1)}, u32[]{:S(2)}, u32[]{:S(2)}) %collective-permute-start.7) | collective-permute-done | bytes 196640 | tf_op jit(solution)/shard_map/ppermute | solution.py:139
  40.8 2.0 %collective-permute-done.8.refs_2_ = bf16[24,4096]{1,0:T(8,128)(2,1)S(1)} collective-permute-done((bf16[24,4096]{1,0:T(8,128)(2,1)S(1)}, bf16[24,4096]{1,0:T(8,128)(2,1)S(1)}, u32[]{:S(2)}, u32[]{:S(2)}) %collective-permute-start.8) | collective-permute-done | bytes 196640 | tf_op jit(solution)/shard_map/ppermute | solution.py:139
  42.8 0.6 %placed.3 = bf16[2,2,4,2,8,4096]{5,4,3,2,1,0:T(8,128)(2,1)S(1)} custom-call(s32[3]{0:T(128)S(1)} %pad_add_fusion.place_ref, bf16[24,4096]{1,0:T(8,128)(2,1)S(1)} %collective-permute-done.6.refs_0_, bf16[24,4096]{1,0:T(8,128)(2,1)S(1)} %collective-permute-done.7.refs_1_, ...), custom_call_target="tpu_custom_call", output_to_operand_aliasing={{}: (7, {})} | custom-call | flops 100000000 | tf_op jit(solution)/shard_map/placed/pallas_call | solution.py:92
  43.5 3.0 %score.1 = f32[256,1024]{1,0:T(8,128)S(1)} custom-call(bf16[256,4096]{1,0:T(8,128)(2,1)S(1)} %bitcast.40, bf16[1024,4096]{1,0:T(8,128)(2,1)S(1)} %bitcast.39), custom_call_target="tpu_custom_call" | custom-call | flops 2147483648 | tf_op jit(solution)/shard_map/score/pallas_call | solution.py:123
  46.7 1.9 %collective-permute-done.15 = f32[2,4,2,8,1024]{4,3,2,1,0:T(8,128)S(1)} collective-permute-done((f32[2,4,2,8,1024]{4,3,2,1,0:T(8,128)S(1)}, f32[2,4,2,8,1024]{4,3,2,1,0:T(8,128)S(1)}, u32[]{:S(2)}, u32[]{:S(2)}) %collective-permute-start.15) | collective-permute-done | bytes 524320 | tf_op jit(solution)/shard_map/ppermute | solution.py:170
  48.6 0.6 %collective-permute-start.16 = (bf16[4,2,8,1024]{3,2,1,0:T(8,128)(2,1)S(1)}, bf16[4,2,8,1024]{3,2,1,0:T(8,128)(2,1)S(1)}, u32[]{:S(2)}, u32[]{:S(2)}) collective-permute-start(bf16[4,2,8,1024]{3,2,1,0:T(8,128)(2,1)S(1)} %fusion.1), channel_id=1, source_target_pairs={{0,128},{64,192},{128,0},{192,64},{1,129},{65,193},{129,1},{193,65... | collective-permute-start | bytes 393224 | tf_op jit(solution)/shard_map/ppermute | solution.py:172
  49.9 8.3 %collective-permute-done.16 = bf16[4,2,8,1024]{3,2,1,0:T(8,128)(2,1)S(1)} collective-permute-done((bf16[4,2,8,1024]{3,2,1,0:T(8,128)(2,1)S(1)}, bf16[4,2,8,1024]{3,2,1,0:T(8,128)(2,1)S(1)}, u32[]{:S(2)}, u32[]{:S(2)}) %collective-permute-start.16) | collective-permute-done | bytes 131104 | tf_op jit(solution)/shard_map/ppermute | solution.py:172
  58.2 0.7 %bitcast_select_fusion = f32[64,1024]{1,0:T(8,128)} fusion(f32[4,2,8,1024]{3,2,1,0:T(8,128)S(1)} %fusion.3, pred[1024]{0:T(1024)(128)(4,1)S(1)} %iota_compare_fusion), kind=kLoop, calls=%fused_computation.8 | loop fusion | flops 65536 | bytes 525312 | tf_op jit(solution)/shard_map/jit(_where)/select_n | solution.py:177
  (35 shorter events, 1.2 us)
Async XLA Ops:
  2.3 4.4 %collective-permute-start = (bf16[4,4096]{1,0:T(4,128)(2,1)S(1)}, bf16[4,4096]{1,0:T(4,128)(2,1)S(1)}, u32[]{:S(2)}, u32[]{:S(2)}) collective-permute-start(bf16[4,4096]{1,0:T(4,128)(2,1)S(1)} %precondition.1), channel_id=1, source_target_pairs={{0,3},{1,2},{2,1},{3,0},{4,7},{5,6},{6,5},{7,4},{8,11},{9,10},{10,... | collective-permute-start | bytes 98312 | tf_op jit(solution)/shard_map/ppermute | solution.py:139
  2.5 6.5 %collective-permute-start.1 = (bf16[4,4096]{1,0:T(4,128)(2,1)S(1)}, bf16[4,4096]{1,0:T(4,128)(2,1)S(1)}, u32[]{:S(2)}, u32[]{:S(2)}) collective-permute-start(bf16[4,4096]{1,0:T(4,128)(2,1)S(1)} %precondition.1), channel_id=1, source_target_pairs={{0,2},{1,3},{2,0},{3,1},{4,6},{5,7},{6,4},{7,5},{8,10},{9,11},{10,... | collective-permute-start | bytes 98312 | tf_op jit(solution)/shard_map/ppermute | solution.py:139
  6.7 3.9 %collective-permute-start.2 = (bf16[4,4096]{1,0:T(4,128)(2,1)S(1)}, bf16[4,4096]{1,0:T(4,128)(2,1)S(1)}, u32[]{:S(2)}, u32[]{:S(2)}) collective-permute-start(bf16[4,4096]{1,0:T(4,128)(2,1)S(1)} %precondition.1), channel_id=1, source_target_pairs={{0,1},{1,0},{2,3},{3,2},{4,5},{5,4},{6,7},{7,6},{8,9},{9,8},{10,11... | collective-permute-start | bytes 98312 | tf_op jit(solution)/shard_map/ppermute | solution.py:139
  10.8 9.4 %collective-permute-start.9 = (bf16[16,4096]{1,0:T(8,128)(2,1)S(1)}, bf16[16,4096]{1,0:T(8,128)(2,1)S(1)}, u32[]{:S(2)}, u32[]{:S(2)}) collective-permute-start(bf16[16,4096]{1,0:T(8,128)(2,1)S(1)} %pad_maximum_fusion.2.refs_0_), channel_id=1, source_target_pairs={{0,4},{1,5},{2,6},{3,7},{4,0},{5,1},{6,2},{7,3},{8,12},{9,13},{10,... | collective-permute-start | bytes 393224 | tf_op jit(solution)/shard_map/ppermute | solution.py:139
  12.4 8.0 %collective-permute-start.10 = (bf16[16,4096]{1,0:T(8,128)(2,1)S(1)}, bf16[16,4096]{1,0:T(8,128)(2,1)S(1)}, u32[]{:S(2)}, u32[]{:S(2)}) collective-permute-start(bf16[16,4096]{1,0:T(8,128)(2,1)S(1)} %pad_maximum_fusion.2.refs_0_), channel_id=1, source_target_pairs={{0,8},{1,9},{2,10},{3,11},{4,12},{5,13},{6,14},{7,15},{8,0},{9,1},... | collective-permute-start | bytes 393224 | tf_op jit(solution)/shard_map/ppermute | solution.py:139
  15.1 6.2 %collective-permute-start.11 = (bf16[16,4096]{1,0:T(8,128)(2,1)S(1)}, bf16[16,4096]{1,0:T(8,128)(2,1)S(1)}, u32[]{:S(2)}, u32[]{:S(2)}) collective-permute-start(bf16[16,4096]{1,0:T(8,128)(2,1)S(1)} %pad_maximum_fusion.2.refs_0_), channel_id=1, source_target_pairs={{0,12},{1,13},{2,14},{3,15},{4,8},{5,9},{6,10},{7,11},{8,4},{9,5},... | collective-permute-start | bytes 393224 | tf_op jit(solution)/shard_map/ppermute | solution.py:139
  15.6 10.2 %collective-permute-start.3 = (bf16[16,4096]{1,0:T(8,128)(2,1)S(1)}, bf16[16,4096]{1,0:T(8,128)(2,1)S(1)}, u32[]{:S(2)}, u32[]{:S(2)}) collective-permute-start(bf16[16,4096]{1,0:T(8,128)(2,1)S(1)} %pad_maximum_fusion.2.refs_0_), channel_id=1, source_target_pairs={{0,16},{1,17},{2,18},{3,19},{4,20},{5,21},{6,22},{7,23},{8,24},{9,... | collective-permute-start | bytes 393224 | tf_op jit(solution)/shard_map/ppermute | solution.py:139
  17.2 8.8 %collective-permute-start.4 = (bf16[16,4096]{1,0:T(8,128)(2,1)S(1)}, bf16[16,4096]{1,0:T(8,128)(2,1)S(1)}, u32[]{:S(2)}, u32[]{:S(2)}) collective-permute-start(bf16[16,4096]{1,0:T(8,128)(2,1)S(1)} %pad_maximum_fusion.2.refs_0_), channel_id=1, source_target_pairs={{0,32},{1,33},{2,34},{3,35},{4,36},{5,37},{6,38},{7,39},{8,40},{9,... | collective-permute-start | bytes 393224 | tf_op jit(solution)/shard_map/ppermute | solution.py:139
  20.1 7.6 %collective-permute-start.5 = (bf16[16,4096]{1,0:T(8,128)(2,1)S(1)}, bf16[16,4096]{1,0:T(8,128)(2,1)S(1)}, u32[]{:S(2)}, u32[]{:S(2)}) collective-permute-start(bf16[16,4096]{1,0:T(8,128)(2,1)S(1)} %pad_maximum_fusion.2.refs_0_), channel_id=1, source_target_pairs={{0,48},{1,49},{2,50},{3,51},{4,52},{5,53},{6,54},{7,55},{8,56},{9,... | collective-permute-start | bytes 393224 | tf_op jit(solution)/shard_map/ppermute | solution.py:139
  21.3 13.7 %collective-permute-start.12 = (bf16[24,4096]{1,0:T(8,128)(2,1)S(1)}, bf16[24,4096]{1,0:T(8,128)(2,1)S(1)}, u32[]{:S(2)}, u32[]{:S(2)}) collective-permute-start(bf16[24,4096]{1,0:T(8,128)(2,1)S(1)} %pad_maximum_fusion.1), channel_id=1, source_target_pairs={{0,16},{1,17},{2,18},{3,19},{4,20},{5,21},{6,22},{7,23},{8,24},{9,... | collective-permute-start | bytes 589832 | tf_op jit(solution)/shard_map/ppermute | solution.py:139
  23.0 12.6 %collective-permute-start.13 = (bf16[24,4096]{1,0:T(8,128)(2,1)S(1)}, bf16[24,4096]{1,0:T(8,128)(2,1)S(1)}, u32[]{:S(2)}, u32[]{:S(2)}) collective-permute-start(bf16[24,4096]{1,0:T(8,128)(2,1)S(1)} %pad_maximum_fusion.1), channel_id=1, source_target_pairs={{0,32},{1,33},{2,34},{3,35},{4,36},{5,37},{6,38},{7,39},{8,40},{9,... | collective-permute-start | bytes 589832 | tf_op jit(solution)/shard_map/ppermute | solution.py:139
  25.9 9.7 %collective-permute-start.14 = (bf16[24,4096]{1,0:T(8,128)(2,1)S(1)}, bf16[24,4096]{1,0:T(8,128)(2,1)S(1)}, u32[]{:S(2)}, u32[]{:S(2)}) collective-permute-start(bf16[24,4096]{1,0:T(8,128)(2,1)S(1)} %pad_maximum_fusion.1), channel_id=1, source_target_pairs={{0,48},{1,49},{2,50},{3,51},{4,52},{5,53},{6,54},{7,55},{8,56},{9,... | collective-permute-start | bytes 589832 | tf_op jit(solution)/shard_map/ppermute | solution.py:139
  27.7 15.7 %slice-start = ((s8[8388608]{0:T(1024)(128)(4,1)}), s8[4194304]{0:T(1024)(128)(4,1)S(1)}, s32[]{:S(2)}) async-start(s8[8388608]{0:T(1024)(128)(4,1)} %bitcast.37), calls=%async_computation | async-start | bytes 8388608
  27.7 15.7 %slice-start.1 = ((s8[8388608]{0:T(1024)(128)(4,1)}), s8[4194304]{0:T(1024)(128)(4,1)S(1)}, s32[]{:S(2)}) async-start(s8[8388608]{0:T(1024)(128)(4,1)} %bitcast.37), calls=%async_computation.1 | async-start | bytes 8388608
  27.7 7.8 %collective-permute-start.6 = (bf16[24,4096]{1,0:T(8,128)(2,1)S(1)}, bf16[24,4096]{1,0:T(8,128)(2,1)S(1)}, u32[]{:S(2)}, u32[]{:S(2)}) collective-permute-start(bf16[24,4096]{1,0:T(8,128)(2,1)S(1)} %pad_maximum_fusion), channel_id=1, source_target_pairs={{0,4},{1,5},{2,6},{3,7},{4,0},{5,1},{6,2},{7,3},{8,12},{9,13},{10,... | collective-permute-start | bytes 589832 | tf_op jit(solution)/shard_map/ppermute | solution.py:139
  28.4 12.4 %collective-permute-start.7 = (bf16[24,4096]{1,0:T(8,128)(2,1)S(1)}, bf16[24,4096]{1,0:T(8,128)(2,1)S(1)}, u32[]{:S(2)}, u32[]{:S(2)}) collective-permute-start(bf16[24,4096]{1,0:T(8,128)(2,1)S(1)} %pad_maximum_fusion), channel_id=1, source_target_pairs={{0,8},{1,9},{2,10},{3,11},{4,12},{5,13},{6,14},{7,15},{8,0},{9,1},... | collective-permute-start | bytes 589832 | tf_op jit(solution)/shard_map/ppermute | solution.py:139
  35.0 7.9 %collective-permute-start.8 = (bf16[24,4096]{1,0:T(8,128)(2,1)S(1)}, bf16[24,4096]{1,0:T(8,128)(2,1)S(1)}, u32[]{:S(2)}, u32[]{:S(2)}) collective-permute-start(bf16[24,4096]{1,0:T(8,128)(2,1)S(1)} %pad_maximum_fusion), channel_id=1, source_target_pairs={{0,12},{1,13},{2,14},{3,15},{4,8},{5,9},{6,10},{7,11},{8,4},{9,5},... | collective-permute-start | bytes 589832 | tf_op jit(solution)/shard_map/ppermute | solution.py:139
  46.6 2.0 %collective-permute-start.15 = (f32[2,4,2,8,1024]{4,3,2,1,0:T(8,128)S(1)}, f32[2,4,2,8,1024]{4,3,2,1,0:T(8,128)S(1)}, u32[]{:S(2)}, u32[]{:S(2)}) collective-permute-start(f32[2,4,2,8,1024]{4,3,2,1,0:T(8,128)S(1)} %bitcast.43), channel_id=1, source_target_pairs={{0,64},{64,0},{128,192},{192,128},{1,65},{65,1},{129,193},{193,129... | collective-permute-start | bytes 1572872 | tf_op jit(solution)/shard_map/ppermute | solution.py:170
  48.6 9.5 %collective-permute-start.16 = (bf16[4,2,8,1024]{3,2,1,0:T(8,128)(2,1)S(1)}, bf16[4,2,8,1024]{3,2,1,0:T(8,128)(2,1)S(1)}, u32[]{:S(2)}, u32[]{:S(2)}) collective-permute-start(bf16[4,2,8,1024]{3,2,1,0:T(8,128)(2,1)S(1)} %fusion.1), channel_id=1, source_target_pairs={{0,128},{64,192},{128,0},{192,64},{1,129},{65,193},{129,1},{193,65... | collective-permute-start | bytes 393224 | tf_op jit(solution)/shard_map/ppermute | solution.py:172
where the time goes:
time: 59 us; the launch traced here: 58.9 us
  starting transfers between devices  26.6 us (45%)
  waiting for transfers between devices  23.8 us (40%)
  Pallas kernels  6.59 us (11%)
  other arithmetic  1.06 us (2%)
  between operations  0.83 us (1%)
    ppermute x15, starting transfers between devices, fetch(): blocks.append(lax.ppermute(block, 'doc', doc_pairs(stride, k)))  25.9 us
    ppermute x15, waiting for transfers between devices, fetch(): blocks.append(lax.ppermute(block, 'doc', doc_pairs(stride, k)))  13.6 us
    ppermute x1, waiting for transfers between devices, on_device(): other_far = lax.ppermute(give, 'layer', layer_pairs(2))  8.27 us
    pallas_call x1, Pallas kernels, score(): pl.pallas_call(score_kernel, out_shape=jax.ShapeDtypeStruct((rows, slots)...  3.03 us
    pallas_call x1, Pallas kernels, precondition(): pl.pallas_call(precondition_kernel, out_shape=jax.ShapeDtypeStruct(gradie...  2.32 us
    ppermute x1, waiting for transfers between devices, on_device(): other = lax.ppermute(tiles[1], 'layer', layer_pairs(1))  1.9 us
    pallas_call x2, Pallas kernels, placed(): pl.pallas_call(functools.partial(place_kernel, tiles), out_shape=jax.Shap...  1.23 us
  transfers between devices with their start and end apart: 17, of which 8 were waited for; matrix products, arithmetic and copies ran while one was open for 0% of the time, Pallas kernels for 1%

commit v1 on v0

--- a/solution.py
+++ b/solution.py
@@ -67,14 +67,18 @@
     + [(0, k, h) for k in (1, 2, 3) for h in range(2)]
     + [(k, 0, h) for k in (1, 2, 3) for h in range(2)]
 )
-diagonal = [(j, i, 0) for i in (1, 2, 3) for j in (1, 2, 3)] + [
-    (j, i, 1) for j in (1, 2, 3) for i in (1, 2, 3)
-]
-
-
-def place_kernel(tiles, place_ref, *refs):
+diagonal = (
+    [t for i in (1, 3) for t in ((2, i, 0), (2, i, 1), (1, i, 0), (1, i, 1), (3, i, 0))]
+    + [(2, 2, 0), (2, 2, 1), (1, 2, 0), (1, 2, 1)]
+    + [(3, 2, 0), (3, 2, 1), (3, 1, 1), (3, 3, 1)]
+)
+
+
+def place_kernel(tiles, *refs):
     out_ref = refs[-1]
-    core_row, far_row, x = place_ref[0], place_ref[1], place_ref[2]
+    doc, layer = lax.axis_index("doc"), lax.axis_index("layer")
+    y, x = doc >> 4, (doc >> 2) & 3
+    core_row, far_row = (y ^ layer) & 1, (y >> 1) ^ (layer >> 1)
     t = 0
     for piece in refs:
         if t == len(tiles):
@@ -85,20 +89,20 @@
             t += 1
 
 
-def placed(tiles, place, pieces, flops, begun=None):
-    vmem, smem = pl.BlockSpec(memory_space=pltpu.VMEM), pl.BlockSpec(memory_space=pltpu.SMEM)
+def placed(tiles, pieces, flops, begun=None):
+    vmem = pl.BlockSpec(memory_space=pltpu.VMEM)
     width = pieces[0].shape[1]
     operands = pieces + ([] if begun is None else [begun])
     return pl.pallas_call(
         functools.partial(place_kernel, tiles),
         out_shape=jax.ShapeDtypeStruct((2, 2, 4, 2, 8, width), jnp.bfloat16),
-        in_specs=[smem] + [vmem] * len(operands),
+        in_specs=[vmem] * len(operands),
         out_specs=vmem,
-        input_output_aliases={} if begun is None else {len(operands): 0},
+        input_output_aliases={} if begun is None else {len(operands) - 1: 0},
         compiler_params=pltpu.CompilerParams(vmem_limit_bytes=8 << 20),
         cost_estimate=pl.CostEstimate(flops=flops, bytes_accessed=0, transcendentals=0),
         name="placed",
-    )(place, *operands)
+    )(*operands)
 
 
 def score_kernel(queries_ref, stored_ref, out_ref):
@@ -133,9 +137,9 @@
     )(queries, stored)
 
 
-def fetch(block, stride):
+def fetch(block, stride, flips=(1, 2, 3)):
     blocks = []
-    for k in (1, 2, 3):
+    for k in flips:
         blocks.append(lax.ppermute(block, "doc", doc_pairs(stride, k)))
     return blocks
 
@@ -148,8 +152,8 @@
 
 
 def on_device(query_grads, stored_grads, basis_in, basis_out, eigen_values, layer_mask, doc_counts):
-    doc, layer = lax.axis_index("doc"), lax.axis_index("layer")
-    y, x, z = doc // 16, (doc // 4) % 4, doc % 4
+    doc = lax.axis_index("doc")
+    z = doc % 4
     stored = pltpu.with_memory_space_constraint(stored_grads[0], pltpu.VMEM)
     own = precondition(
         query_grads[0], basis_in[0], basis_out[0], eigen_values[0], layer_mask[:, 0], doc
@@ -158,13 +162,17 @@
     rows = ordered([own] + fetch(own, 1), z)
     block = lax.optimization_barrier(jnp.concatenate(rows, axis=0))
     along_y, along_x = fetch(block, 16), fetch(block, 4)
-    core, far = layer & 1, layer >> 1
-    place = jnp.stack([(y & 1) ^ core, (y >> 1) ^ far, x]).astype(jnp.int32)
-    queries = placed(straight, place, [block] + along_x + along_y, 2 * 10**10)
-    upper = jnp.concatenate([b[:8] for b in along_y])
-    lower = jnp.concatenate([b[8:] for b in along_x])
-    diagonals = fetch(upper, 4) + fetch(lower, 16)
-    queries = placed(diagonal, place, diagonals, 10**8, queries)
+    queries = placed(straight, [block] + along_x + along_y, 2 * 10**10)
+    (y1, y2, y3), (x1, x2, x3) = along_y, along_x
+    upper = jnp.concatenate([y2, y1, y3[:8]])
+    lower = jnp.concatenate([x2, x1[8:], x3[8:]])
+    diagonals = (
+        fetch(upper, 4, (1, 3))
+        + fetch(y2, 4, (2,))
+        + fetch(x2, 16, (1,))
+        + fetch(lower, 16, (3,))
+    )
+    queries = placed(diagonal, diagonals, 10**8, queries)
     tiles = score(queries.reshape(256, -1), stored)
     tiles = tiles.reshape(2, 2, 4, 2, 8, -1)
     other = lax.ppermute(tiles[1], "layer", layer_pairs(1))

time: 59 us -> 55.2 us (0.936)
  the two profiles are of different devices: /device:TPU:64 before, /device:TPU:74 now
where the time goes in v1:
time: 55.2 us; the launch traced here: 55 us
  starting transfers between devices  27.2 us (49%)
  waiting for transfers between devices  20.5 us (37%)
  Pallas kernels  5.45 us (10%)
  other arithmetic  1.03 us (2%)
  between operations  0.78 us (1%)
    ppermute x14, starting transfers between devices, fetch(): blocks.append(lax.ppermute(block, 'doc', doc_pairs(stride, k)))  22.4 us
    ppermute x14, waiting for transfers between devices, fetch(): blocks.append(lax.ppermute(block, 'doc', doc_pairs(stride, k)))  11.6 us
    ppermute x1, waiting for transfers between devices, on_device(): other_far = lax.ppermute(give, 'layer', layer_pairs(2))  7.02 us
    ppermute x1, starting transfers between devices, on_device(): other_far = lax.ppermute(give, 'layer', layer_pairs(2))  4.7 us
    pallas_call x1, Pallas kernels, score(): pl.pallas_call(score_kernel, out_shape=jax.ShapeDtypeStruct((rows, slots)...  2.96 us
    pallas_call x1, Pallas kernels, precondition(): pl.pallas_call(precondition_kernel, out_shape=jax.ShapeDtypeStruct(gradie...  2.32 us
    ppermute x1, waiting for transfers between devices, on_device(): other = lax.ppermute(tiles[1], 'layer', layer_pairs(1))  1.9 us
  transfers between devices with their start and end apart: 16, of which 8 were waited for; matrix products, arithmetic and copies ran while one was open for 0% of the time, Pallas kernels for 0%

profile of v1, /device:TPU:74, one launch (start us, length us, event | category | flops | bytes accessed | tf_op | source)
XLA Modules:
  0.0 55.0 jit_solution(17946547343957910684)
XLA Ops:
  0.0 2.3 %precondition.1 = bf16[4,4096]{1,0:T(4,128)(2,1)S(1)} custom-call(s32[256]{0:T(256)} %bitcast.45, s32[1]{0:T(128)} %bitcast.2.doc_ref, bf16[4,4096]{1,0:T(4,128)(2,1)} %bitcast.41, f32[64,64]{1,0:T(8,128)} %bitcast.42, f32[64,64]{1,0:T(8,128)} %bitcast.43, f32[64,64]{1,0:T(8,128)} %bitcast.44), custom_call_target="tpu_custom_call" | custom-call | tf_op jit(solution)/shard_map/precondition/pallas_call | solution.py:55
  2.5 4.2 %collective-permute-start.1 = (bf16[4,4096]{1,0:T(4,128)(2,1)S(1)}, bf16[4,4096]{1,0:T(4,128)(2,1)S(1)}, u32[]{:S(2)}, u32[]{:S(2)}) collective-permute-start(bf16[4,4096]{1,0:T(4,128)(2,1)S(1)} %precondition.1), channel_id=1, source_target_pairs={{0,2},{1,3},{2,0},{3,1},{4,6},{5,7},{6,4},{7,5},{8,10},{9,11},{10,... | collective-permute-start | bytes 98312 | tf_op jit(solution)/shard_map/ppermute | solution.py:143
  6.7 2.2 %collective-permute-done.1 = bf16[4,4096]{1,0:T(4,128)(2,1)S(1)} collective-permute-done((bf16[4,4096]{1,0:T(4,128)(2,1)S(1)}, bf16[4,4096]{1,0:T(4,128)(2,1)S(1)}, u32[]{:S(2)}, u32[]{:S(2)}) %collective-permute-start.1) | collective-permute-done | bytes 32800 | tf_op jit(solution)/shard_map/ppermute | solution.py:143
  8.9 1.7 %collective-permute-done.2 = bf16[4,4096]{1,0:T(4,128)(2,1)S(1)} collective-permute-done((bf16[4,4096]{1,0:T(4,128)(2,1)S(1)}, bf16[4,4096]{1,0:T(4,128)(2,1)S(1)}, u32[]{:S(2)}, u32[]{:S(2)}) %collective-permute-start.2) | collective-permute-done | bytes 32800 | tf_op jit(solution)/shard_map/ppermute | solution.py:143
  10.8 1.7 %collective-permute-start.5 = (bf16[16,4096]{1,0:T(8,128)(2,1)S(1)}, bf16[16,4096]{1,0:T(8,128)(2,1)S(1)}, u32[]{:S(2)}, u32[]{:S(2)}) collective-permute-start(bf16[16,4096]{1,0:T(8,128)(2,1)S(1)} %pad_maximum_fusion.2.refs_0_), channel_id=1, source_target_pairs={{0,48},{1,49},{2,50},{3,51},{4,52},{5,53},{6,54},{7,55},{8,56},{9,... | collective-permute-start | bytes 393224 | tf_op jit(solution)/shard_map/ppermute | solution.py:143
  12.4 0.9 %collective-permute-start.3 = (bf16[16,4096]{1,0:T(8,128)(2,1)S(1)}, bf16[16,4096]{1,0:T(8,128)(2,1)S(1)}, u32[]{:S(2)}, u32[]{:S(2)}) collective-permute-start(bf16[16,4096]{1,0:T(8,128)(2,1)S(1)} %pad_maximum_fusion.2.refs_0_), channel_id=1, source_target_pairs={{0,32},{1,33},{2,34},{3,35},{4,36},{5,37},{6,38},{7,39},{8,40},{9,... | collective-permute-start | bytes 393224 | tf_op jit(solution)/shard_map/ppermute | solution.py:143
  13.4 1.6 %collective-permute-start.4 = (bf16[16,4096]{1,0:T(8,128)(2,1)S(1)}, bf16[16,4096]{1,0:T(8,128)(2,1)S(1)}, u32[]{:S(2)}, u32[]{:S(2)}) collective-permute-start(bf16[16,4096]{1,0:T(8,128)(2,1)S(1)} %pad_maximum_fusion.2.refs_0_), channel_id=1, source_target_pairs={{0,16},{1,17},{2,18},{3,19},{4,20},{5,21},{6,22},{7,23},{8,24},{9,... | collective-permute-start | bytes 393224 | tf_op jit(solution)/shard_map/ppermute | solution.py:143
  15.0 0.5 collective-permute-start.11
  15.5 2.2 %collective-permute-start.12 = (bf16[16,4096]{1,0:T(8,128)(2,1)S(1)}, bf16[16,4096]{1,0:T(8,128)(2,1)S(1)}, u32[]{:S(2)}, u32[]{:S(2)}) collective-permute-start(bf16[16,4096]{1,0:T(8,128)(2,1)S(1)} %pad_maximum_fusion.2.refs_0_), channel_id=1, source_target_pairs={{0,12},{1,13},{2,14},{3,15},{4,8},{5,9},{6,10},{7,11},{8,4},{9,5},... | collective-permute-start | bytes 393224 | tf_op jit(solution)/shard_map/ppermute | solution.py:143
  17.7 1.7 %collective-permute-start.9 = (bf16[16,4096]{1,0:T(8,128)(2,1)S(1)}, bf16[16,4096]{1,0:T(8,128)(2,1)S(1)}, u32[]{:S(2)}, u32[]{:S(2)}) collective-permute-start(bf16[16,4096]{1,0:T(8,128)(2,1)S(1)} %pad_maximum_fusion.2.refs_0_), channel_id=1, source_target_pairs={{0,8},{1,9},{2,10},{3,11},{4,12},{5,13},{6,14},{7,15},{8,0},{9,1},... | collective-permute-start | bytes 393224 | tf_op jit(solution)/shard_map/ppermute | solution.py:143
  19.4 1.5 %collective-permute-start.6 = (bf16[40,4096]{1,0:T(8,128)(2,1)S(1)}, bf16[40,4096]{1,0:T(8,128)(2,1)S(1)}, u32[]{:S(2)}, u32[]{:S(2)}) collective-permute-start(bf16[40,4096]{1,0:T(8,128)(2,1)S(1)} %pad_maximum_fusion), channel_id=1, source_target_pairs={{0,4},{1,5},{2,6},{3,7},{4,0},{5,1},{6,2},{7,3},{8,12},{9,13},{10,... | collective-permute-start | bytes 983048 | tf_op jit(solution)/shard_map/ppermute | solution.py:143
  20.9 1.2 %collective-permute-start.7 = (bf16[40,4096]{1,0:T(8,128)(2,1)S(1)}, bf16[40,4096]{1,0:T(8,128)(2,1)S(1)}, u32[]{:S(2)}, u32[]{:S(2)}) collective-permute-start(bf16[40,4096]{1,0:T(8,128)(2,1)S(1)} %pad_maximum_fusion), channel_id=1, source_target_pairs={{0,12},{1,13},{2,14},{3,15},{4,8},{5,9},{6,10},{7,11},{8,4},{9,5},... | collective-permute-start | bytes 983048 | tf_op jit(solution)/shard_map/ppermute | solution.py:143
  22.1 0.6 %collective-permute-done.12.refs_3_ = bf16[16,4096]{1,0:T(8,128)(2,1)S(1)} collective-permute-done((bf16[16,4096]{1,0:T(8,128)(2,1)S(1)}, bf16[16,4096]{1,0:T(8,128)(2,1)S(1)}, u32[]{:S(2)}, u32[]{:S(2)}) %collective-permute-start.12) | collective-permute-done | bytes 131104 | tf_op jit(solution)/shard_map/ppermute | solution.py:143
  22.7 2.8 %collective-permute-done.9.refs_2_ = bf16[16,4096]{1,0:T(8,128)(2,1)S(1)} collective-permute-done((bf16[16,4096]{1,0:T(8,128)(2,1)S(1)}, bf16[16,4096]{1,0:T(8,128)(2,1)S(1)}, u32[]{:S(2)}, u32[]{:S(2)}) %collective-permute-start.9) | collective-permute-done | bytes 131104 | tf_op jit(solution)/shard_map/ppermute | solution.py:143
  25.6 1.7 %collective-permute-start.13 = (bf16[32,4096]{1,0:T(8,128)(2,1)S(1)}, bf16[32,4096]{1,0:T(8,128)(2,1)S(1)}, u32[]{:S(2)}, u32[]{:S(2)}) collective-permute-start(bf16[32,4096]{1,0:T(8,128)(2,1)S(1)} %pad_maximum_fusion.1), channel_id=1, source_target_pairs={{0,48},{1,49},{2,50},{3,51},{4,52},{5,53},{6,54},{7,55},{8,56},{9,... | collective-permute-start | bytes 786440 | tf_op jit(solution)/shard_map/ppermute | solution.py:143
  27.2 2.9 %collective-permute-start.10 = (bf16[16,4096]{1,0:T(8,128)(2,1)S(1)}, bf16[16,4096]{1,0:T(8,128)(2,1)S(1)}, u32[]{:S(2)}, u32[]{:S(2)}) collective-permute-start(bf16[16,4096]{1,0:T(8,128)(2,1)S(1)} %collective-permute-done.9.refs_2_), channel_id=1, source_target_pairs={{0,16},{1,17},{2,18},{3,19},{4,20},{5,21},{6,22},{7,23},{8,24},{9,... | collective-permute-start | bytes 393224 | tf_op jit(solution)/shard_map/ppermute | solution.py:143
  30.2 2.1 %collective-permute-start.8 = (bf16[16,4096]{1,0:T(8,128)(2,1)S(1)}, bf16[16,4096]{1,0:T(8,128)(2,1)S(1)}, u32[]{:S(2)}, u32[]{:S(2)}) collective-permute-start(bf16[16,4096]{1,0:T(8,128)(2,1)S(1)} %collective-permute-done.3.refs_5_), channel_id=1, source_target_pairs={{0,8},{1,9},{2,10},{3,11},{4,12},{5,13},{6,14},{7,15},{8,0},{9,1},... | collective-permute-start | bytes 393224 | tf_op jit(solution)/shard_map/ppermute | solution.py:143
  32.4 0.7 %collective-permute-done.10.refs_3_ = bf16[16,4096]{1,0:T(8,128)(2,1)S(1)} collective-permute-done((bf16[16,4096]{1,0:T(8,128)(2,1)S(1)}, bf16[16,4096]{1,0:T(8,128)(2,1)S(1)}, u32[]{:S(2)}, u32[]{:S(2)}) %collective-permute-start.10) | collective-permute-done | bytes 131104 | tf_op jit(solution)/shard_map/ppermute | solution.py:143
  33.1 3.5 %collective-permute-done.8.refs_2_ = bf16[16,4096]{1,0:T(8,128)(2,1)S(1)} collective-permute-done((bf16[16,4096]{1,0:T(8,128)(2,1)S(1)}, bf16[16,4096]{1,0:T(8,128)(2,1)S(1)}, u32[]{:S(2)}, u32[]{:S(2)}) %collective-permute-start.8) | collective-permute-done | bytes 131104 | tf_op jit(solution)/shard_map/ppermute | solution.py:143
  36.8 3.0 %score.1 = f32[256,1024]{1,0:T(8,128)S(1)} custom-call(bf16[256,4096]{1,0:T(8,128)(2,1)S(1)} %bitcast.37, bf16[1024,4096]{1,0:T(8,128)(2,1)S(1)} %bitcast.36), custom_call_target="tpu_custom_call" | custom-call | flops 2147483648 | tf_op jit(solution)/shard_map/score/pallas_call | solution.py:127
  39.9 1.9 %collective-permute-done.14 = f32[2,4,2,8,1024]{4,3,2,1,0:T(8,128)S(1)} collective-permute-done((f32[2,4,2,8,1024]{4,3,2,1,0:T(8,128)S(1)}, f32[2,4,2,8,1024]{4,3,2,1,0:T(8,128)S(1)}, u32[]{:S(2)}, u32[]{:S(2)}) %collective-permute-start.14) | collective-permute-done | bytes 524320 | tf_op jit(solution)/shard_map/ppermute | solution.py:178
  41.8 4.7 %collective-permute-start.15 = (bf16[4,2,8,1024]{3,2,1,0:T(8,128)(2,1)S(1)}, bf16[4,2,8,1024]{3,2,1,0:T(8,128)(2,1)S(1)}, u32[]{:S(2)}, u32[]{:S(2)}) collective-permute-start(bf16[4,2,8,1024]{3,2,1,0:T(8,128)(2,1)S(1)} %fusion.1), channel_id=1, source_target_pairs={{0,128},{64,192},{128,0},{192,64},{1,129},{65,193},{129,1},{193,65... | collective-permute-start | bytes 393224 | tf_op jit(solution)/shard_map/ppermute | solution.py:180
  47.2 7.0 %collective-permute-done.15 = bf16[4,2,8,1024]{3,2,1,0:T(8,128)(2,1)S(1)} collective-permute-done((bf16[4,2,8,1024]{3,2,1,0:T(8,128)(2,1)S(1)}, bf16[4,2,8,1024]{3,2,1,0:T(8,128)(2,1)S(1)}, u32[]{:S(2)}, u32[]{:S(2)}) %collective-permute-start.15) | collective-permute-done | bytes 131104 | tf_op jit(solution)/shard_map/ppermute | solution.py:180
  54.3 0.7 %bitcast_select_fusion = f32[64,1024]{1,0:T(8,128)} fusion(f32[4,2,8,1024]{3,2,1,0:T(8,128)S(1)} %fusion.3, pred[1024]{0:T(1024)(128)(4,1)S(1)} %iota_compare_fusion), kind=kLoop, calls=%fused_computation.10 | loop fusion | flops 65536 | bytes 525312 | tf_op jit(solution)/shard_map/jit(_where)/select_n | solution.py:185
  (29 shorter events, 0.8 us)
Async XLA Ops:
  2.3 4.4 %collective-permute-start = (bf16[4,4096]{1,0:T(4,128)(2,1)S(1)}, bf16[4,4096]{1,0:T(4,128)(2,1)S(1)}, u32[]{:S(2)}, u32[]{:S(2)}) collective-permute-start(bf16[4,4096]{1,0:T(4,128)(2,1)S(1)} %precondition.1), channel_id=1, source_target_pairs={{0,3},{1,2},{2,1},{3,0},{4,7},{5,6},{6,5},{7,4},{8,11},{9,10},{10,... | collective-permute-start | bytes 98312 | tf_op jit(solution)/shard_map/ppermute | solution.py:143
  2.5 6.4 %collective-permute-start.1 = (bf16[4,4096]{1,0:T(4,128)(2,1)S(1)}, bf16[4,4096]{1,0:T(4,128)(2,1)S(1)}, u32[]{:S(2)}, u32[]{:S(2)}) collective-permute-start(bf16[4,4096]{1,0:T(4,128)(2,1)S(1)} %precondition.1), channel_id=1, source_target_pairs={{0,2},{1,3},{2,0},{3,1},{4,6},{5,7},{6,4},{7,5},{8,10},{9,11},{10,... | collective-permute-start | bytes 98312 | tf_op jit(solution)/shard_map/ppermute | solution.py:143
  6.7 3.9 %collective-permute-start.2 = (bf16[4,4096]{1,0:T(4,128)(2,1)S(1)}, bf16[4,4096]{1,0:T(4,128)(2,1)S(1)}, u32[]{:S(2)}, u32[]{:S(2)}) collective-permute-start(bf16[4,4096]{1,0:T(4,128)(2,1)S(1)} %precondition.1), channel_id=1, source_target_pairs={{0,1},{1,0},{2,3},{3,2},{4,5},{5,4},{6,7},{7,6},{8,9},{9,8},{10,11... | collective-permute-start | bytes 98312 | tf_op jit(solution)/shard_map/ppermute | solution.py:143
  10.8 6.9 %collective-permute-start.5 = (bf16[16,4096]{1,0:T(8,128)(2,1)S(1)}, bf16[16,4096]{1,0:T(8,128)(2,1)S(1)}, u32[]{:S(2)}, u32[]{:S(2)}) collective-permute-start(bf16[16,4096]{1,0:T(8,128)(2,1)S(1)} %pad_maximum_fusion.2.refs_0_), channel_id=1, source_target_pairs={{0,48},{1,49},{2,50},{3,51},{4,52},{5,53},{6,54},{7,55},{8,56},{9,... | collective-permute-start | bytes 393224 | tf_op jit(solution)/shard_map/ppermute | solution.py:143
  12.4 6.9 %collective-permute-start.3 = (bf16[16,4096]{1,0:T(8,128)(2,1)S(1)}, bf16[16,4096]{1,0:T(8,128)(2,1)S(1)}, u32[]{:S(2)}, u32[]{:S(2)}) collective-permute-start(bf16[16,4096]{1,0:T(8,128)(2,1)S(1)} %pad_maximum_fusion.2.refs_0_), channel_id=1, source_target_pairs={{0,32},{1,33},{2,34},{3,35},{4,36},{5,37},{6,38},{7,39},{8,40},{9,... | collective-permute-start | bytes 393224 | tf_op jit(solution)/shard_map/ppermute | solution.py:143
  13.4 6.0 %collective-permute-start.4 = (bf16[16,4096]{1,0:T(8,128)(2,1)S(1)}, bf16[16,4096]{1,0:T(8,128)(2,1)S(1)}, u32[]{:S(2)}, u32[]{:S(2)}) collective-permute-start(bf16[16,4096]{1,0:T(8,128)(2,1)S(1)} %pad_maximum_fusion.2.refs_0_), channel_id=1, source_target_pairs={{0,16},{1,17},{2,18},{3,19},{4,20},{5,21},{6,22},{7,23},{8,24},{9,... | collective-permute-start | bytes 393224 | tf_op jit(solution)/shard_map/ppermute | solution.py:143
  15.0 7.2 %collective-permute-start.11 = (bf16[16,4096]{1,0:T(8,128)(2,1)S(1)}, bf16[16,4096]{1,0:T(8,128)(2,1)S(1)}, u32[]{:S(2)}, u32[]{:S(2)}) collective-permute-start(bf16[16,4096]{1,0:T(8,128)(2,1)S(1)} %pad_maximum_fusion.2.refs_0_), channel_id=1, source_target_pairs={{0,4},{1,5},{2,6},{3,7},{4,0},{5,1},{6,2},{7,3},{8,12},{9,13},{10,... | collective-permute-start | bytes 393224 | tf_op jit(solution)/shard_map/ppermute | solution.py:143
  15.5 7.2 %collective-permute-start.12 = (bf16[16,4096]{1,0:T(8,128)(2,1)S(1)}, bf16[16,4096]{1,0:T(8,128)(2,1)S(1)}, u32[]{:S(2)}, u32[]{:S(2)}) collective-permute-start(bf16[16,4096]{1,0:T(8,128)(2,1)S(1)} %pad_maximum_fusion.2.refs_0_), channel_id=1, source_target_pairs={{0,12},{1,13},{2,14},{3,15},{4,8},{5,9},{6,10},{7,11},{8,4},{9,5},... | collective-permute-start | bytes 393224 | tf_op jit(solution)/shard_map/ppermute | solution.py:143
  17.7 7.9 %collective-permute-start.9 = (bf16[16,4096]{1,0:T(8,128)(2,1)S(1)}, bf16[16,4096]{1,0:T(8,128)(2,1)S(1)}, u32[]{:S(2)}, u32[]{:S(2)}) collective-permute-start(bf16[16,4096]{1,0:T(8,128)(2,1)S(1)} %pad_maximum_fusion.2.refs_0_), channel_id=1, source_target_pairs={{0,8},{1,9},{2,10},{3,11},{4,12},{5,13},{6,14},{7,15},{8,0},{9,1},... | collective-permute-start | bytes 393224 | tf_op jit(solution)/shard_map/ppermute | solution.py:143
  19.4 17.2 %collective-permute-start.6 = (bf16[40,4096]{1,0:T(8,128)(2,1)S(1)}, bf16[40,4096]{1,0:T(8,128)(2,1)S(1)}, u32[]{:S(2)}, u32[]{:S(2)}) collective-permute-start(bf16[40,4096]{1,0:T(8,128)(2,1)S(1)} %pad_maximum_fusion), channel_id=1, source_target_pairs={{0,4},{1,5},{2,6},{3,7},{4,0},{5,1},{6,2},{7,3},{8,12},{9,13},{10,... | collective-permute-start | bytes 983048 | tf_op jit(solution)/shard_map/ppermute | solution.py:143
  20.9 15.7 %collective-permute-start.7 = (bf16[40,4096]{1,0:T(8,128)(2,1)S(1)}, bf16[40,4096]{1,0:T(8,128)(2,1)S(1)}, u32[]{:S(2)}, u32[]{:S(2)}) collective-permute-start(bf16[40,4096]{1,0:T(8,128)(2,1)S(1)} %pad_maximum_fusion), channel_id=1, source_target_pairs={{0,12},{1,13},{2,14},{3,15},{4,8},{5,9},{6,10},{7,11},{8,4},{9,5},... | collective-permute-start | bytes 983048 | tf_op jit(solution)/shard_map/ppermute | solution.py:143
  25.5 11.2 %slice-start = ((s8[8388608]{0:T(1024)(128)(4,1)}), s8[4194304]{0:T(1024)(128)(4,1)S(1)}, s32[]{:S(2)}) async-start(s8[8388608]{0:T(1024)(128)(4,1)} %bitcast.34), calls=%async_computation | async-start | bytes 8388608
  25.6 11.2 %slice-start.1 = ((s8[8388608]{0:T(1024)(128)(4,1)}), s8[4194304]{0:T(1024)(128)(4,1)S(1)}, s32[]{:S(2)}) async-start(s8[8388608]{0:T(1024)(128)(4,1)} %bitcast.34), calls=%async_computation.1 | async-start | bytes 8388608
  25.6 11.1 %collective-permute-start.13 = (bf16[32,4096]{1,0:T(8,128)(2,1)S(1)}, bf16[32,4096]{1,0:T(8,128)(2,1)S(1)}, u32[]{:S(2)}, u32[]{:S(2)}) collective-permute-start(bf16[32,4096]{1,0:T(8,128)(2,1)S(1)} %pad_maximum_fusion.1), channel_id=1, source_target_pairs={{0,48},{1,49},{2,50},{3,51},{4,52},{5,53},{6,54},{7,55},{8,56},{9,... | collective-permute-start | bytes 786440 | tf_op jit(solution)/shard_map/ppermute | solution.py:143
  27.2 5.9 %collective-permute-start.10 = (bf16[16,4096]{1,0:T(8,128)(2,1)S(1)}, bf16[16,4096]{1,0:T(8,128)(2,1)S(1)}, u32[]{:S(2)}, u32[]{:S(2)}) collective-permute-start(bf16[16,4096]{1,0:T(8,128)(2,1)S(1)} %collective-permute-done.9.refs_2_), channel_id=1, source_target_pairs={{0,16},{1,17},{2,18},{3,19},{4,20},{5,21},{6,22},{7,23},{8,24},{9,... | collective-permute-start | bytes 393224 | tf_op jit(solution)/shard_map/ppermute | solution.py:143
  30.2 6.5 %collective-permute-start.8 = (bf16[16,4096]{1,0:T(8,128)(2,1)S(1)}, bf16[16,4096]{1,0:T(8,128)(2,1)S(1)}, u32[]{:S(2)}, u32[]{:S(2)}) collective-permute-start(bf16[16,4096]{1,0:T(8,128)(2,1)S(1)} %collective-permute-done.3.refs_5_), channel_id=1, source_target_pairs={{0,8},{1,9},{2,10},{3,11},{4,12},{5,13},{6,14},{7,15},{8,0},{9,1},... | collective-permute-start | bytes 393224 | tf_op jit(solution)/shard_map/ppermute | solution.py:143
  39.8 2.0 %collective-permute-start.14 = (f32[2,4,2,8,1024]{4,3,2,1,0:T(8,128)S(1)}, f32[2,4,2,8,1024]{4,3,2,1,0:T(8,128)S(1)}, u32[]{:S(2)}, u32[]{:S(2)}) collective-permute-start(f32[2,4,2,8,1024]{4,3,2,1,0:T(8,128)S(1)} %bitcast.40), channel_id=1, source_target_pairs={{0,64},{64,0},{128,192},{192,128},{1,65},{65,1},{129,193},{193,129... | collective-permute-start | bytes 1572872 | tf_op jit(solution)/shard_map/ppermute | solution.py:178
  41.8 12.4 %collective-permute-start.15 = (bf16[4,2,8,1024]{3,2,1,0:T(8,128)(2,1)S(1)}, bf16[4,2,8,1024]{3,2,1,0:T(8,128)(2,1)S(1)}, u32[]{:S(2)}, u32[]{:S(2)}) collective-permute-start(bf16[4,2,8,1024]{3,2,1,0:T(8,128)(2,1)S(1)} %fusion.1), channel_id=1, source_target_pairs={{0,128},{64,192},{128,0},{192,64},{1,129},{65,193},{129,1},{193,65... | collective-permute-start | bytes 393224 | tf_op jit(solution)/shard_map/ppermute | solution.py:180

commit v2 on v1

--- a/solution.py
+++ b/solution.py
@@ -20,13 +20,18 @@
     return [(l, l ^ flip) for l in range(4)]
 
 
+def halves(a):
+    high = a.astype(jnp.bfloat16)
+    return high, (a - high.astype(jnp.float32)).astype(jnp.bfloat16)
+
+
 def exact_dot(a, b, dims):
-    return lax.dot_general(
-        a, b, (dims, ((), ())), precision=lax.Precision.HIGHEST, preferred_element_type=jnp.float32
-    )
-
-
-def precondition_kernel(mask_ref, doc_ref, grads_ref, basis_in_ref, basis_out_ref, eigen_ref, out_ref):
+    (a_high, a_low), (b_high, b_low) = halves(a), halves(b)
+    dot = lambda p, q: lax.dot_general(p, q, (dims, ((), ())), preferred_element_type=jnp.float32)
+    return dot(a_high, b_high) + (dot(a_high, b_low) + dot(a_low, b_high))
+
+
+def precondition_kernel(mask_ref, grads_ref, basis_in_ref, basis_out_ref, eigen_ref, out_ref):
     count, out_size, in_size = grads_ref.shape[0], basis_out_ref.shape[0], basis_in_ref.shape[0]
     base_in, base_out = basis_in_ref[...], basis_out_ref[...]
     divisor = eigen_ref[...] + damping
@@ -41,12 +46,12 @@
     restored = exact_dot(base_out, side_by_side, ((1,), (0,)))
     rows = []
     for q, block in enumerate(jnp.split(restored, count, axis=1)):
-        weight = mask_ref[doc_ref[0] * count + q].astype(jnp.float32)
+        weight = mask_ref[lax.axis_index("doc") * count + q].astype(jnp.float32)
         rows.append(block * weight)
     out_ref[...] = jnp.stack(rows).reshape(count, out_size * in_size).astype(jnp.bfloat16)
 
 
-def precondition(gradients, basis_in, basis_out, eigen_values, mask, doc):
+def precondition(gradients, basis_in, basis_out, eigen_values, mask):
     vmem, smem = pl.BlockSpec(memory_space=pltpu.VMEM), pl.BlockSpec(memory_space=pltpu.SMEM)
     operands = [
         pltpu.with_memory_space_constraint(a, pltpu.HBM)
@@ -55,11 +60,11 @@
     return pl.pallas_call(
         precondition_kernel,
         out_shape=jax.ShapeDtypeStruct(gradients.shape, jnp.bfloat16),
-        in_specs=[smem, smem, vmem, vmem, vmem, vmem],
+        in_specs=[smem, vmem, vmem, vmem, vmem],
         out_specs=vmem,
         compiler_params=pltpu.CompilerParams(vmem_limit_bytes=4 << 20),
         name="precondition",
-    )(operands[0], doc.reshape(1), *operands[1:])
+    )(*operands)
 
 
 straight = (
@@ -106,7 +111,7 @@
 
 
 def score_kernel(queries_ref, stored_ref, out_ref):
-    width = 256
+    width = 1024
 
     def tile(i, carry):
         columns = pl.ds(pl.multiple_of(i * width, width), width)
@@ -156,7 +161,7 @@
     z = doc % 4
     stored = pltpu.with_memory_space_constraint(stored_grads[0], pltpu.VMEM)
     own = precondition(
-        query_grads[0], basis_in[0], basis_out[0], eigen_values[0], layer_mask[:, 0], doc
+        query_grads[0], basis_in[0], basis_out[0], eigen_values[0], layer_mask[:, 0]
     )
 
     rows = ordered([own] + fetch(own, 1), z)

time: 55.2 us -> 54.2 us (0.982)
  the two profiles are of different devices: /device:TPU:74 before, /device:TPU:78 now
where the time goes in v2:
time: 54.2 us; the launch traced here: 54.1 us
  starting transfers between devices  25.7 us (47%)
  waiting for transfers between devices  22 us (41%)
  Pallas kernels  4.53 us (8%)
  other arithmetic  1.02 us (2%)
  between operations  0.77 us (1%)
    ppermute x14, starting transfers between devices, fetch(): blocks.append(lax.ppermute(block, 'doc', doc_pairs(stride, k)))  20.9 us
    ppermute x14, waiting for transfers between devices, fetch(): blocks.append(lax.ppermute(block, 'doc', doc_pairs(stride, k)))  13.1 us
    ppermute x1, waiting for transfers between devices, on_device(): other_far = lax.ppermute(give, 'layer', layer_pairs(2))  7.02 us
    ppermute x1, starting transfers between devices, on_device(): other_far = lax.ppermute(give, 'layer', layer_pairs(2))  4.71 us
    pallas_call x1, Pallas kernels, score(): pl.pallas_call(score_kernel, out_shape=jax.ShapeDtypeStruct((rows, slots)...  2.36 us
    pallas_call x1, Pallas kernels, precondition(): pl.pallas_call(precondition_kernel, out_shape=jax.ShapeDtypeStruct(gradie...  2.01 us
    ppermute x1, waiting for transfers between devices, on_device(): other = lax.ppermute(tiles[1], 'layer', layer_pairs(1))  1.9 us
  transfers between devices with their start and end apart: 16, of which 10 were waited for; matrix products, arithmetic and copies ran while one was open for 0% of the time, Pallas kernels for 0%

profile of v2, /device:TPU:78, one launch (start us, length us, event | category | flops | bytes accessed | tf_op | source)
XLA Modules:
  0.0 54.1 jit_solution(7342692689203430624)
XLA Ops:
  0.0 2.0 %precondition.1 = bf16[4,4096]{1,0:T(4,128)(2,1)S(1)} custom-call(s32[256]{0:T(256)} %bitcast.44, bf16[4,4096]{1,0:T(4,128)(2,1)} %bitcast.40, f32[64,64]{1,0:T(8,128)} %bitcast.41, f32[64,64]{1,0:T(8,128)} %bitcast.42, f32[64,64]{1,0:T(8,128)} %bitcast.43), custom_call_target="tpu_custom_call" | custom-call | tf_op jit(solution)/shard_map/precondition/pallas_call | solution.py:60
  2.2 4.2 %collective-permute-start.1 = (bf16[4,4096]{1,0:T(4,128)(2,1)S(1)}, bf16[4,4096]{1,0:T(4,128)(2,1)S(1)}, u32[]{:S(2)}, u32[]{:S(2)}) collective-permute-start(bf16[4,4096]{1,0:T(4,128)(2,1)S(1)} %precondition.1), channel_id=1, source_target_pairs={{0,2},{1,3},{2,0},{3,1},{4,6},{5,7},{6,4},{7,5},{8,10},{9,11},{10,... | collective-permute-start | bytes 98312 | tf_op jit(solution)/shard_map/ppermute | solution.py:148
  6.4 2.2 %collective-permute-done.1 = bf16[4,4096]{1,0:T(4,128)(2,1)S(1)} collective-permute-done((bf16[4,4096]{1,0:T(4,128)(2,1)S(1)}, bf16[4,4096]{1,0:T(4,128)(2,1)S(1)}, u32[]{:S(2)}, u32[]{:S(2)}) %collective-permute-start.1) | collective-permute-done | bytes 32800 | tf_op jit(solution)/shard_map/ppermute | solution.py:148
  8.6 1.7 %collective-permute-done.2 = bf16[4,4096]{1,0:T(4,128)(2,1)S(1)} collective-permute-done((bf16[4,4096]{1,0:T(4,128)(2,1)S(1)}, bf16[4,4096]{1,0:T(4,128)(2,1)S(1)}, u32[]{:S(2)}, u32[]{:S(2)}) %collective-permute-start.2) | collective-permute-done | bytes 32800 | tf_op jit(solution)/shard_map/ppermute | solution.py:148
  10.5 1.7 %collective-permute-start.5 = (bf16[16,4096]{1,0:T(8,128)(2,1)S(1)}, bf16[16,4096]{1,0:T(8,128)(2,1)S(1)}, u32[]{:S(2)}, u32[]{:S(2)}) collective-permute-start(bf16[16,4096]{1,0:T(8,128)(2,1)S(1)} %pad_maximum_fusion.2.refs_0_), channel_id=1, source_target_pairs={{0,48},{1,49},{2,50},{3,51},{4,52},{5,53},{6,54},{7,55},{8,56},{9,... | collective-permute-start | bytes 393224 | tf_op jit(solution)/shard_map/ppermute | solution.py:148
  12.1 0.9 %collective-permute-start.3 = (bf16[16,4096]{1,0:T(8,128)(2,1)S(1)}, bf16[16,4096]{1,0:T(8,128)(2,1)S(1)}, u32[]{:S(2)}, u32[]{:S(2)}) collective-permute-start(bf16[16,4096]{1,0:T(8,128)(2,1)S(1)} %pad_maximum_fusion.2.refs_0_), channel_id=1, source_target_pairs={{0,32},{1,33},{2,34},{3,35},{4,36},{5,37},{6,38},{7,39},{8,40},{9,... | collective-permute-start | bytes 393224 | tf_op jit(solution)/shard_map/ppermute | solution.py:148
  13.1 1.6 %collective-permute-start.4 = (bf16[16,4096]{1,0:T(8,128)(2,1)S(1)}, bf16[16,4096]{1,0:T(8,128)(2,1)S(1)}, u32[]{:S(2)}, u32[]{:S(2)}) collective-permute-start(bf16[16,4096]{1,0:T(8,128)(2,1)S(1)} %pad_maximum_fusion.2.refs_0_), channel_id=1, source_target_pairs={{0,16},{1,17},{2,18},{3,19},{4,20},{5,21},{6,22},{7,23},{8,24},{9,... | collective-permute-start | bytes 393224 | tf_op jit(solution)/shard_map/ppermute | solution.py:148
  14.6 0.8 %collective-permute-start.11 = (bf16[16,4096]{1,0:T(8,128)(2,1)S(1)}, bf16[16,4096]{1,0:T(8,128)(2,1)S(1)}, u32[]{:S(2)}, u32[]{:S(2)}) collective-permute-start(bf16[16,4096]{1,0:T(8,128)(2,1)S(1)} %pad_maximum_fusion.2.refs_0_), channel_id=1, source_target_pairs={{0,4},{1,5},{2,6},{3,7},{4,0},{5,1},{6,2},{7,3},{8,12},{9,13},{10,... | collective-permute-start | bytes 393224 | tf_op jit(solution)/shard_map/ppermute | solution.py:148
  15.5 1.1 %collective-permute-start.12 = (bf16[16,4096]{1,0:T(8,128)(2,1)S(1)}, bf16[16,4096]{1,0:T(8,128)(2,1)S(1)}, u32[]{:S(2)}, u32[]{:S(2)}) collective-permute-start(bf16[16,4096]{1,0:T(8,128)(2,1)S(1)} %pad_maximum_fusion.2.refs_0_), channel_id=1, source_target_pairs={{0,12},{1,13},{2,14},{3,15},{4,8},{5,9},{6,10},{7,11},{8,4},{9,5},... | collective-permute-start | bytes 393224 | tf_op jit(solution)/shard_map/ppermute | solution.py:148
  16.9 1.8 %collective-permute-start.9 = (bf16[16,4096]{1,0:T(8,128)(2,1)S(1)}, bf16[16,4096]{1,0:T(8,128)(2,1)S(1)}, u32[]{:S(2)}, u32[]{:S(2)}) collective-permute-start(bf16[16,4096]{1,0:T(8,128)(2,1)S(1)} %pad_maximum_fusion.2.refs_0_), channel_id=1, source_target_pairs={{0,8},{1,9},{2,10},{3,11},{4,12},{5,13},{6,14},{7,15},{8,0},{9,1},... | collective-permute-start | bytes 393224 | tf_op jit(solution)/shard_map/ppermute | solution.py:148
  19.0 0.9 %collective-permute-start.6 = (bf16[40,4096]{1,0:T(8,128)(2,1)S(1)}, bf16[40,4096]{1,0:T(8,128)(2,1)S(1)}, u32[]{:S(2)}, u32[]{:S(2)}) collective-permute-start(bf16[40,4096]{1,0:T(8,128)(2,1)S(1)} %pad_maximum_fusion), channel_id=1, source_target_pairs={{0,4},{1,5},{2,6},{3,7},{4,0},{5,1},{6,2},{7,3},{8,12},{9,13},{10,... | collective-permute-start | bytes 983048 | tf_op jit(solution)/shard_map/ppermute | solution.py:148
  19.9 1.2 %collective-permute-start.7 = (bf16[40,4096]{1,0:T(8,128)(2,1)S(1)}, bf16[40,4096]{1,0:T(8,128)(2,1)S(1)}, u32[]{:S(2)}, u32[]{:S(2)}) collective-permute-start(bf16[40,4096]{1,0:T(8,128)(2,1)S(1)} %pad_maximum_fusion), channel_id=1, source_target_pairs={{0,12},{1,13},{2,14},{3,15},{4,8},{5,9},{6,10},{7,11},{8,4},{9,5},... | collective-permute-start | bytes 983048 | tf_op jit(solution)/shard_map/ppermute | solution.py:148
  21.2 1.9 %collective-permute-done.12.refs_3_ = bf16[16,4096]{1,0:T(8,128)(2,1)S(1)} collective-permute-done((bf16[16,4096]{1,0:T(8,128)(2,1)S(1)}, bf16[16,4096]{1,0:T(8,128)(2,1)S(1)}, u32[]{:S(2)}, u32[]{:S(2)}) %collective-permute-start.12) | collective-permute-done | bytes 131104 | tf_op jit(solution)/shard_map/ppermute | solution.py:148
  23.1 1.7 %collective-permute-done.9.refs_2_ = bf16[16,4096]{1,0:T(8,128)(2,1)S(1)} collective-permute-done((bf16[16,4096]{1,0:T(8,128)(2,1)S(1)}, bf16[16,4096]{1,0:T(8,128)(2,1)S(1)}, u32[]{:S(2)}, u32[]{:S(2)}) %collective-permute-start.9) | collective-permute-done | bytes 131104 | tf_op jit(solution)/shard_map/ppermute | solution.py:148
  24.8 1.4 %collective-permute-start.13 = (bf16[32,4096]{1,0:T(8,128)(2,1)S(1)}, bf16[32,4096]{1,0:T(8,128)(2,1)S(1)}, u32[]{:S(2)}, u32[]{:S(2)}) collective-permute-start(bf16[32,4096]{1,0:T(8,128)(2,1)S(1)} %pad_maximum_fusion.1), channel_id=1, source_target_pairs={{0,48},{1,49},{2,50},{3,51},{4,52},{5,53},{6,54},{7,55},{8,56},{9,... | collective-permute-start | bytes 786440 | tf_op jit(solution)/shard_map/ppermute | solution.py:148
  26.2 3.7 %collective-permute-start.10 = (bf16[16,4096]{1,0:T(8,128)(2,1)S(1)}, bf16[16,4096]{1,0:T(8,128)(2,1)S(1)}, u32[]{:S(2)}, u32[]{:S(2)}) collective-permute-start(bf16[16,4096]{1,0:T(8,128)(2,1)S(1)} %collective-permute-done.9.refs_2_), channel_id=1, source_target_pairs={{0,16},{1,17},{2,18},{3,19},{4,20},{5,21},{6,22},{7,23},{8,24},{9,... | collective-permute-start | bytes 393224 | tf_op jit(solution)/shard_map/ppermute | solution.py:148
  29.9 1.4 %collective-permute-start.8 = (bf16[16,4096]{1,0:T(8,128)(2,1)S(1)}, bf16[16,4096]{1,0:T(8,128)(2,1)S(1)}, u32[]{:S(2)}, u32[]{:S(2)}) collective-permute-start(bf16[16,4096]{1,0:T(8,128)(2,1)S(1)} %collective-permute-done.3.refs_5_), channel_id=1, source_target_pairs={{0,8},{1,9},{2,10},{3,11},{4,12},{5,13},{6,14},{7,15},{8,0},{9,1},... | collective-permute-start | bytes 393224 | tf_op jit(solution)/shard_map/ppermute | solution.py:148
  31.3 1.5 %collective-permute-done.10.refs_3_ = bf16[16,4096]{1,0:T(8,128)(2,1)S(1)} collective-permute-done((bf16[16,4096]{1,0:T(8,128)(2,1)S(1)}, bf16[16,4096]{1,0:T(8,128)(2,1)S(1)}, u32[]{:S(2)}, u32[]{:S(2)}) %collective-permute-start.10) | collective-permute-done | bytes 131104 | tf_op jit(solution)/shard_map/ppermute | solution.py:148
  32.8 3.5 %collective-permute-done.8.refs_2_ = bf16[16,4096]{1,0:T(8,128)(2,1)S(1)} collective-permute-done((bf16[16,4096]{1,0:T(8,128)(2,1)S(1)}, bf16[16,4096]{1,0:T(8,128)(2,1)S(1)}, u32[]{:S(2)}, u32[]{:S(2)}) %collective-permute-start.8) | collective-permute-done | bytes 131104 | tf_op jit(solution)/shard_map/ppermute | solution.py:148
  36.5 2.4 %score.1 = f32[256,1024]{1,0:T(8,128)S(1)} custom-call(bf16[256,4096]{1,0:T(8,128)(2,1)S(1)} %bitcast.36, bf16[1024,4096]{1,0:T(8,128)(2,1)S(1)} %bitcast.35), custom_call_target="tpu_custom_call" | custom-call | flops 2147483648 | tf_op jit(solution)/shard_map/score/pallas_call | solution.py:132
  39.0 1.9 %collective-permute-done.14 = f32[2,4,2,8,1024]{4,3,2,1,0:T(8,128)S(1)} collective-permute-done((f32[2,4,2,8,1024]{4,3,2,1,0:T(8,128)S(1)}, f32[2,4,2,8,1024]{4,3,2,1,0:T(8,128)S(1)}, u32[]{:S(2)}, u32[]{:S(2)}) %collective-permute-start.14) | collective-permute-done | bytes 524320 | tf_op jit(solution)/shard_map/ppermute | solution.py:183
  40.9 4.7 %collective-permute-start.15 = (bf16[4,2,8,1024]{3,2,1,0:T(8,128)(2,1)S(1)}, bf16[4,2,8,1024]{3,2,1,0:T(8,128)(2,1)S(1)}, u32[]{:S(2)}, u32[]{:S(2)}) collective-permute-start(bf16[4,2,8,1024]{3,2,1,0:T(8,128)(2,1)S(1)} %fusion.1), channel_id=1, source_target_pairs={{0,128},{64,192},{128,0},{192,64},{1,129},{65,193},{129,1},{193,65... | collective-permute-start | bytes 393224 | tf_op jit(solution)/shard_map/ppermute | solution.py:185
  46.3 7.0 %collective-permute-done.15 = bf16[4,2,8,1024]{3,2,1,0:T(8,128)(2,1)S(1)} collective-permute-done((bf16[4,2,8,1024]{3,2,1,0:T(8,128)(2,1)S(1)}, bf16[4,2,8,1024]{3,2,1,0:T(8,128)(2,1)S(1)}, u32[]{:S(2)}, u32[]{:S(2)}) %collective-permute-start.15) | collective-permute-done | bytes 131104 | tf_op jit(solution)/shard_map/ppermute | solution.py:185
  53.4 0.7 %bitcast_select_fusion = f32[64,1024]{1,0:T(8,128)} fusion(f32[4,2,8,1024]{3,2,1,0:T(8,128)S(1)} %fusion.3, pred[1024]{0:T(1024)(128)(4,1)S(1)} %iota_compare_fusion), kind=kLoop, calls=%fused_computation.10 | loop fusion | flops 65536 | bytes 525312 | tf_op jit(solution)/shard_map/jit(_where)/select_n | solution.py:190
  (29 shorter events, 1.4 us)
Async XLA Ops:
  2.0 4.4 %collective-permute-start = (bf16[4,4096]{1,0:T(4,128)(2,1)S(1)}, bf16[4,4096]{1,0:T(4,128)(2,1)S(1)}, u32[]{:S(2)}, u32[]{:S(2)}) collective-permute-start(bf16[4,4096]{1,0:T(4,128)(2,1)S(1)} %precondition.1), channel_id=1, source_target_pairs={{0,3},{1,2},{2,1},{3,0},{4,7},{5,6},{6,5},{7,4},{8,11},{9,10},{10,... | collective-permute-start | bytes 98312 | tf_op jit(solution)/shard_map/ppermute | solution.py:148
  2.2 6.4 %collective-permute-start.1 = (bf16[4,4096]{1,0:T(4,128)(2,1)S(1)}, bf16[4,4096]{1,0:T(4,128)(2,1)S(1)}, u32[]{:S(2)}, u32[]{:S(2)}) collective-permute-start(bf16[4,4096]{1,0:T(4,128)(2,1)S(1)} %precondition.1), channel_id=1, source_target_pairs={{0,2},{1,3},{2,0},{3,1},{4,6},{5,7},{6,4},{7,5},{8,10},{9,11},{10,... | collective-permute-start | bytes 98312 | tf_op jit(solution)/shard_map/ppermute | solution.py:148
  6.4 3.9 %collective-permute-start.2 = (bf16[4,4096]{1,0:T(4,128)(2,1)S(1)}, bf16[4,4096]{1,0:T(4,128)(2,1)S(1)}, u32[]{:S(2)}, u32[]{:S(2)}) collective-permute-start(bf16[4,4096]{1,0:T(4,128)(2,1)S(1)} %precondition.1), channel_id=1, source_target_pairs={{0,1},{1,0},{2,3},{3,2},{4,5},{5,4},{6,7},{7,6},{8,9},{9,8},{10,11... | collective-permute-start | bytes 98312 | tf_op jit(solution)/shard_map/ppermute | solution.py:148
  10.5 6.5 %collective-permute-start.5 = (bf16[16,4096]{1,0:T(8,128)(2,1)S(1)}, bf16[16,4096]{1,0:T(8,128)(2,1)S(1)}, u32[]{:S(2)}, u32[]{:S(2)}) collective-permute-start(bf16[16,4096]{1,0:T(8,128)(2,1)S(1)} %pad_maximum_fusion.2.refs_0_), channel_id=1, source_target_pairs={{0,48},{1,49},{2,50},{3,51},{4,52},{5,53},{6,54},{7,55},{8,56},{9,... | collective-permute-start | bytes 393224 | tf_op jit(solution)/shard_map/ppermute | solution.py:148
  12.1 6.6 %collective-permute-start.3 = (bf16[16,4096]{1,0:T(8,128)(2,1)S(1)}, bf16[16,4096]{1,0:T(8,128)(2,1)S(1)}, u32[]{:S(2)}, u32[]{:S(2)}) collective-permute-start(bf16[16,4096]{1,0:T(8,128)(2,1)S(1)} %pad_maximum_fusion.2.refs_0_), channel_id=1, source_target_pairs={{0,32},{1,33},{2,34},{3,35},{4,36},{5,37},{6,38},{7,39},{8,40},{9,... | collective-permute-start | bytes 393224 | tf_op jit(solution)/shard_map/ppermute | solution.py:148
  13.1 5.9 %collective-permute-start.4 = (bf16[16,4096]{1,0:T(8,128)(2,1)S(1)}, bf16[16,4096]{1,0:T(8,128)(2,1)S(1)}, u32[]{:S(2)}, u32[]{:S(2)}) collective-permute-start(bf16[16,4096]{1,0:T(8,128)(2,1)S(1)} %pad_maximum_fusion.2.refs_0_), channel_id=1, source_target_pairs={{0,16},{1,17},{2,18},{3,19},{4,20},{5,21},{6,22},{7,23},{8,24},{9,... | collective-permute-start | bytes 393224 | tf_op jit(solution)/shard_map/ppermute | solution.py:148
  14.6 6.5 %collective-permute-start.11 = (bf16[16,4096]{1,0:T(8,128)(2,1)S(1)}, bf16[16,4096]{1,0:T(8,128)(2,1)S(1)}, u32[]{:S(2)}, u32[]{:S(2)}) collective-permute-start(bf16[16,4096]{1,0:T(8,128)(2,1)S(1)} %pad_maximum_fusion.2.refs_0_), channel_id=1, source_target_pairs={{0,4},{1,5},{2,6},{3,7},{4,0},{5,1},{6,2},{7,3},{8,12},{9,13},{10,... | collective-permute-start | bytes 393224 | tf_op jit(solution)/shard_map/ppermute | solution.py:148
  15.5 7.6 %collective-permute-start.12 = (bf16[16,4096]{1,0:T(8,128)(2,1)S(1)}, bf16[16,4096]{1,0:T(8,128)(2,1)S(1)}, u32[]{:S(2)}, u32[]{:S(2)}) collective-permute-start(bf16[16,4096]{1,0:T(8,128)(2,1)S(1)} %pad_maximum_fusion.2.refs_0_), channel_id=1, source_target_pairs={{0,12},{1,13},{2,14},{3,15},{4,8},{5,9},{6,10},{7,11},{8,4},{9,5},... | collective-permute-start | bytes 393224 | tf_op jit(solution)/shard_map/ppermute | solution.py:148
  16.9 7.9 %collective-permute-start.9 = (bf16[16,4096]{1,0:T(8,128)(2,1)S(1)}, bf16[16,4096]{1,0:T(8,128)(2,1)S(1)}, u32[]{:S(2)}, u32[]{:S(2)}) collective-permute-start(bf16[16,4096]{1,0:T(8,128)(2,1)S(1)} %pad_maximum_fusion.2.refs_0_), channel_id=1, source_target_pairs={{0,8},{1,9},{2,10},{3,11},{4,12},{5,13},{6,14},{7,15},{8,0},{9,1},... | collective-permute-start | bytes 393224 | tf_op jit(solution)/shard_map/ppermute | solution.py:148
  19.0 17.3 %collective-permute-start.6 = (bf16[40,4096]{1,0:T(8,128)(2,1)S(1)}, bf16[40,4096]{1,0:T(8,128)(2,1)S(1)}, u32[]{:S(2)}, u32[]{:S(2)}) collective-permute-start(bf16[40,4096]{1,0:T(8,128)(2,1)S(1)} %pad_maximum_fusion), channel_id=1, source_target_pairs={{0,4},{1,5},{2,6},{3,7},{4,0},{5,1},{6,2},{7,3},{8,12},{9,13},{10,... | collective-permute-start | bytes 983048 | tf_op jit(solution)/shard_map/ppermute | solution.py:148
  19.9 16.4 %collective-permute-start.7 = (bf16[40,4096]{1,0:T(8,128)(2,1)S(1)}, bf16[40,4096]{1,0:T(8,128)(2,1)S(1)}, u32[]{:S(2)}, u32[]{:S(2)}) collective-permute-start(bf16[40,4096]{1,0:T(8,128)(2,1)S(1)} %pad_maximum_fusion), channel_id=1, source_target_pairs={{0,12},{1,13},{2,14},{3,15},{4,8},{5,9},{6,10},{7,11},{8,4},{9,5},... | collective-permute-start | bytes 983048 | tf_op jit(solution)/shard_map/ppermute | solution.py:148
  24.8 11.6 %slice-start = ((s8[8388608]{0:T(1024)(128)(4,1)}), s8[4194304]{0:T(1024)(128)(4,1)S(1)}, s32[]{:S(2)}) async-start(s8[8388608]{0:T(1024)(128)(4,1)} %bitcast.33), calls=%async_computation | async-start | bytes 8388608
  24.8 11.6 %slice-start.1 = ((s8[8388608]{0:T(1024)(128)(4,1)}), s8[4194304]{0:T(1024)(128)(4,1)S(1)}, s32[]{:S(2)}) async-start(s8[8388608]{0:T(1024)(128)(4,1)} %bitcast.33), calls=%async_computation.1 | async-start | bytes 8388608
  24.8 11.5 %collective-permute-start.13 = (bf16[32,4096]{1,0:T(8,128)(2,1)S(1)}, bf16[32,4096]{1,0:T(8,128)(2,1)S(1)}, u32[]{:S(2)}, u32[]{:S(2)}) collective-permute-start(bf16[32,4096]{1,0:T(8,128)(2,1)S(1)} %pad_maximum_fusion.1), channel_id=1, source_target_pairs={{0,48},{1,49},{2,50},{3,51},{4,52},{5,53},{6,54},{7,55},{8,56},{9,... | collective-permute-start | bytes 786440 | tf_op jit(solution)/shard_map/ppermute | solution.py:148
  26.2 6.6 %collective-permute-start.10 = (bf16[16,4096]{1,0:T(8,128)(2,1)S(1)}, bf16[16,4096]{1,0:T(8,128)(2,1)S(1)}, u32[]{:S(2)}, u32[]{:S(2)}) collective-permute-start(bf16[16,4096]{1,0:T(8,128)(2,1)S(1)} %collective-permute-done.9.refs_2_), channel_id=1, source_target_pairs={{0,16},{1,17},{2,18},{3,19},{4,20},{5,21},{6,22},{7,23},{8,24},{9,... | collective-permute-start | bytes 393224 | tf_op jit(solution)/shard_map/ppermute | solution.py:148
  29.9 6.5 %collective-permute-start.8 = (bf16[16,4096]{1,0:T(8,128)(2,1)S(1)}, bf16[16,4096]{1,0:T(8,128)(2,1)S(1)}, u32[]{:S(2)}, u32[]{:S(2)}) collective-permute-start(bf16[16,4096]{1,0:T(8,128)(2,1)S(1)} %collective-permute-done.3.refs_5_), channel_id=1, source_target_pairs={{0,8},{1,9},{2,10},{3,11},{4,12},{5,13},{6,14},{7,15},{8,0},{9,1},... | collective-permute-start | bytes 393224 | tf_op jit(solution)/shard_map/ppermute | solution.py:148
  38.9 2.0 %collective-permute-start.14 = (f32[2,4,2,8,1024]{4,3,2,1,0:T(8,128)S(1)}, f32[2,4,2,8,1024]{4,3,2,1,0:T(8,128)S(1)}, u32[]{:S(2)}, u32[]{:S(2)}) collective-permute-start(f32[2,4,2,8,1024]{4,3,2,1,0:T(8,128)S(1)} %bitcast.39), channel_id=1, source_target_pairs={{0,64},{64,0},{128,192},{192,128},{1,65},{65,1},{129,193},{193,129... | collective-permute-start | bytes 1572872 | tf_op jit(solution)/shard_map/ppermute | solution.py:183
  40.9 12.4 %collective-permute-start.15 = (bf16[4,2,8,1024]{3,2,1,0:T(8,128)(2,1)S(1)}, bf16[4,2,8,1024]{3,2,1,0:T(8,128)(2,1)S(1)}, u32[]{:S(2)}, u32[]{:S(2)}) collective-permute-start(bf16[4,2,8,1024]{3,2,1,0:T(8,128)(2,1)S(1)} %fusion.1), channel_id=1, source_target_pairs={{0,128},{64,192},{128,0},{192,64},{1,129},{65,193},{129,1},{193,65... | collective-permute-start | bytes 393224 | tf_op jit(solution)/shard_map/ppermute | solution.py:185

commit v3 on v2

--- a/solution.py
+++ b/solution.py
@@ -73,9 +73,9 @@
     + [(k, 0, h) for k in (1, 2, 3) for h in range(2)]
 )
 diagonal = (
-    [t for i in (1, 3) for t in ((2, i, 0), (2, i, 1), (1, i, 0), (1, i, 1), (3, i, 0))]
-    + [(2, 2, 0), (2, 2, 1), (1, 2, 0), (1, 2, 1)]
-    + [(3, 2, 0), (3, 2, 1), (3, 1, 1), (3, 3, 1)]
+    [t for j in (1, 3) for t in ((j, 2, 0), (j, 2, 1), (j, 1, 0), (j, 1, 1), (j, 3, 1))]
+    + [(2, 2, 0), (2, 2, 1), (2, 1, 0), (2, 1, 1)]
+    + [(2, 3, 0), (2, 3, 1), (1, 3, 0), (3, 3, 0)]
 )
 
 
@@ -169,13 +169,13 @@
     along_y, along_x = fetch(block, 16), fetch(block, 4)
     queries = placed(straight, [block] + along_x + along_y, 2 * 10**10)
     (y1, y2, y3), (x1, x2, x3) = along_y, along_x
-    upper = jnp.concatenate([y2, y1, y3[:8]])
-    lower = jnp.concatenate([x2, x1[8:], x3[8:]])
+    upper = jnp.concatenate([y2, y1[:8], y3[:8]])
+    lower = jnp.concatenate([x2, x1, x3[8:]])
     diagonals = (
-        fetch(upper, 4, (1, 3))
-        + fetch(y2, 4, (2,))
-        + fetch(x2, 16, (1,))
-        + fetch(lower, 16, (3,))
+        fetch(lower, 16, (1, 3))
+        + fetch(x2, 16, (2,))
+        + fetch(y2, 4, (1,))
+        + fetch(upper, 4, (3,))
     )
     queries = placed(diagonal, diagonals, 10**8, queries)
     tiles = score(queries.reshape(256, -1), stored)

time: 54.2 us -> 54.2 us (level)
  the two profiles are of different devices: /device:TPU:78 before, /device:TPU:6 now
where the time goes in v3:
time: 54.2 us; the launch traced here: 54.1 us
  starting transfers between devices  26.6 us (49%)
  waiting for transfers between devices  21.1 us (39%)
  Pallas kernels  4.52 us (8%)
  other arithmetic  1.03 us (2%)
  between operations  0.78 us (1%)
    ppermute x14, starting transfers between devices, fetch(): blocks.append(lax.ppermute(block, 'doc', doc_pairs(stride, k)))  21.6 us
    ppermute x14, waiting for transfers between devices, fetch(): blocks.append(lax.ppermute(block, 'doc', doc_pairs(stride, k)))  12.9 us
    ppermute x1, waiting for transfers between devices, on_device(): other_far = lax.ppermute(give, 'layer', layer_pairs(2))  6.34 us
    ppermute x1, starting transfers between devices, on_device(): other_far = lax.ppermute(give, 'layer', layer_pairs(2))  4.9 us
    pallas_call x1, Pallas kernels, score(): pl.pallas_call(score_kernel, out_shape=jax.ShapeDtypeStruct((rows, slots)...  2.35 us
    pallas_call x1, Pallas kernels, precondition(): pl.pallas_call(precondition_kernel, out_shape=jax.ShapeDtypeStruct(gradie...  2.01 us
    ppermute x1, waiting for transfers between devices, on_device(): other = lax.ppermute(tiles[1], 'layer', layer_pairs(1))  1.9 us
  transfers between devices with their start and end apart: 16, of which 10 were waited for; matrix products, arithmetic and copies ran while one was open for 0% of the time, Pallas kernels for 0%

profile of v3, /device:TPU:6, one launch (start us, length us, event | category | flops | bytes accessed | tf_op | source)
XLA Modules:
  0.0 54.1 jit_solution(14665166650407040652)
XLA Ops:
  0.0 2.0 %precondition.1 = bf16[4,4096]{1,0:T(4,128)(2,1)S(1)} custom-call(s32[256]{0:T(256)} %bitcast.44, bf16[4,4096]{1,0:T(4,128)(2,1)} %bitcast.40, f32[64,64]{1,0:T(8,128)} %bitcast.41, f32[64,64]{1,0:T(8,128)} %bitcast.42, f32[64,64]{1,0:T(8,128)} %bitcast.43), custom_call_target="tpu_custom_call" | custom-call | tf_op jit(solution)/shard_map/precondition/pallas_call | solution.py:60
  2.0 4.7 %collective-permute-start = (bf16[4,4096]{1,0:T(4,128)(2,1)S(1)}, bf16[4,4096]{1,0:T(4,128)(2,1)S(1)}, u32[]{:S(2)}, u32[]{:S(2)}) collective-permute-start(bf16[4,4096]{1,0:T(4,128)(2,1)S(1)} %precondition.1), channel_id=1, source_target_pairs={{0,3},{1,2},{2,1},{3,0},{4,7},{5,6},{6,5},{7,4},{8,11},{9,10},{10,... | collective-permute-start | bytes 98312 | tf_op jit(solution)/shard_map/ppermute | solution.py:148
  6.7 0.7 %collective-permute-start.2 = (bf16[4,4096]{1,0:T(4,128)(2,1)S(1)}, bf16[4,4096]{1,0:T(4,128)(2,1)S(1)}, u32[]{:S(2)}, u32[]{:S(2)}) collective-permute-start(bf16[4,4096]{1,0:T(4,128)(2,1)S(1)} %precondition.1), channel_id=1, source_target_pairs={{0,1},{1,0},{2,3},{3,2},{4,5},{5,4},{6,7},{7,6},{8,9},{9,8},{10,11... | collective-permute-start | bytes 98312 | tf_op jit(solution)/shard_map/ppermute | solution.py:148
  7.4 1.4 %collective-permute-done = bf16[4,4096]{1,0:T(4,128)(2,1)S(1)} collective-permute-done((bf16[4,4096]{1,0:T(4,128)(2,1)S(1)}, bf16[4,4096]{1,0:T(4,128)(2,1)S(1)}, u32[]{:S(2)}, u32[]{:S(2)}) %collective-permute-start) | collective-permute-done | bytes 32800 | tf_op jit(solution)/shard_map/ppermute | solution.py:148
  8.8 2.7 %collective-permute-done.1 = bf16[4,4096]{1,0:T(4,128)(2,1)S(1)} collective-permute-done((bf16[4,4096]{1,0:T(4,128)(2,1)S(1)}, bf16[4,4096]{1,0:T(4,128)(2,1)S(1)}, u32[]{:S(2)}, u32[]{:S(2)}) %collective-permute-start.1) | collective-permute-done | bytes 32800 | tf_op jit(solution)/shard_map/ppermute | solution.py:148
  11.7 0.6 %collective-permute-start.5 = (bf16[16,4096]{1,0:T(8,128)(2,1)S(1)}, bf16[16,4096]{1,0:T(8,128)(2,1)S(1)}, u32[]{:S(2)}, u32[]{:S(2)}) collective-permute-start(bf16[16,4096]{1,0:T(8,128)(2,1)S(1)} %pad_maximum_fusion.2.refs_0_), channel_id=1, source_target_pairs={{0,12},{1,13},{2,14},{3,15},{4,8},{5,9},{6,10},{7,11},{8,4},{9,5},... | collective-permute-start | bytes 393224 | tf_op jit(solution)/shard_map/ppermute | solution.py:148
  12.3 2.4 %collective-permute-start.3 = (bf16[16,4096]{1,0:T(8,128)(2,1)S(1)}, bf16[16,4096]{1,0:T(8,128)(2,1)S(1)}, u32[]{:S(2)}, u32[]{:S(2)}) collective-permute-start(bf16[16,4096]{1,0:T(8,128)(2,1)S(1)} %pad_maximum_fusion.2.refs_0_), channel_id=1, source_target_pairs={{0,8},{1,9},{2,10},{3,11},{4,12},{5,13},{6,14},{7,15},{8,0},{9,1},... | collective-permute-start | bytes 393224 | tf_op jit(solution)/shard_map/ppermute | solution.py:148
  14.7 1.2 %collective-permute-start.4 = (bf16[16,4096]{1,0:T(8,128)(2,1)S(1)}, bf16[16,4096]{1,0:T(8,128)(2,1)S(1)}, u32[]{:S(2)}, u32[]{:S(2)}) collective-permute-start(bf16[16,4096]{1,0:T(8,128)(2,1)S(1)} %pad_maximum_fusion.2.refs_0_), channel_id=1, source_target_pairs={{0,4},{1,5},{2,6},{3,7},{4,0},{5,1},{6,2},{7,3},{8,12},{9,13},{10,... | collective-permute-start | bytes 393224 | tf_op jit(solution)/shard_map/ppermute | solution.py:148
  15.9 1.6 %collective-permute-start.11 = (bf16[16,4096]{1,0:T(8,128)(2,1)S(1)}, bf16[16,4096]{1,0:T(8,128)(2,1)S(1)}, u32[]{:S(2)}, u32[]{:S(2)}) collective-permute-start(bf16[16,4096]{1,0:T(8,128)(2,1)S(1)} %pad_maximum_fusion.2.refs_0_), channel_id=1, source_target_pairs={{0,16},{1,17},{2,18},{3,19},{4,20},{5,21},{6,22},{7,23},{8,24},{9,... | collective-permute-start | bytes 393224 | tf_op jit(solution)/shard_map/ppermute | solution.py:148
  17.5 2.2 %collective-permute-start.12 = (bf16[16,4096]{1,0:T(8,128)(2,1)S(1)}, bf16[16,4096]{1,0:T(8,128)(2,1)S(1)}, u32[]{:S(2)}, u32[]{:S(2)}) collective-permute-start(bf16[16,4096]{1,0:T(8,128)(2,1)S(1)} %pad_maximum_fusion.2.refs_0_), channel_id=1, source_target_pairs={{0,48},{1,49},{2,50},{3,51},{4,52},{5,53},{6,54},{7,55},{8,56},{9,... | collective-permute-start | bytes 393224 | tf_op jit(solution)/shard_map/ppermute | solution.py:148
  20.0 3.2 %collective-permute-start.9 = (bf16[16,4096]{1,0:T(8,128)(2,1)S(1)}, bf16[16,4096]{1,0:T(8,128)(2,1)S(1)}, u32[]{:S(2)}, u32[]{:S(2)}) collective-permute-start(bf16[16,4096]{1,0:T(8,128)(2,1)S(1)} %pad_maximum_fusion.2.refs_0_), channel_id=1, source_target_pairs={{0,32},{1,33},{2,34},{3,35},{4,36},{5,37},{6,38},{7,39},{8,40},{9,... | collective-permute-start | bytes 393224 | tf_op jit(solution)/shard_map/ppermute | solution.py:148
  23.2 0.8 %collective-permute-start.6 = (bf16[40,4096]{1,0:T(8,128)(2,1)S(1)}, bf16[40,4096]{1,0:T(8,128)(2,1)S(1)}, u32[]{:S(2)}, u32[]{:S(2)}) collective-permute-start(bf16[40,4096]{1,0:T(8,128)(2,1)S(1)} %pad_maximum_fusion), channel_id=1, source_target_pairs={{0,16},{1,17},{2,18},{3,19},{4,20},{5,21},{6,22},{7,23},{8,24},{9,... | collective-permute-start | bytes 983048 | tf_op jit(solution)/shard_map/ppermute | solution.py:148
  24.5 0.6 %collective-permute-done.12.refs_6_ = bf16[16,4096]{1,0:T(8,128)(2,1)S(1)} collective-permute-done((bf16[16,4096]{1,0:T(8,128)(2,1)S(1)}, bf16[16,4096]{1,0:T(8,128)(2,1)S(1)}, u32[]{:S(2)}, u32[]{:S(2)}) %collective-permute-start.12) | collective-permute-done | bytes 131104 | tf_op jit(solution)/shard_map/ppermute | solution.py:148
  25.1 2.4 %collective-permute-done.9.refs_5_ = bf16[16,4096]{1,0:T(8,128)(2,1)S(1)} collective-permute-done((bf16[16,4096]{1,0:T(8,128)(2,1)S(1)}, bf16[16,4096]{1,0:T(8,128)(2,1)S(1)}, u32[]{:S(2)}, u32[]{:S(2)}) %collective-permute-start.9) | collective-permute-done | bytes 131104 | tf_op jit(solution)/shard_map/ppermute | solution.py:148
  27.5 0.6 %collective-permute-start.13 = (bf16[32,4096]{1,0:T(8,128)(2,1)S(1)}, bf16[32,4096]{1,0:T(8,128)(2,1)S(1)}, u32[]{:S(2)}, u32[]{:S(2)}) collective-permute-start(bf16[32,4096]{1,0:T(8,128)(2,1)S(1)} %pad_maximum_fusion.1), channel_id=1, source_target_pairs={{0,12},{1,13},{2,14},{3,15},{4,8},{5,9},{6,10},{7,11},{8,4},{9,5},... | collective-permute-start | bytes 786440 | tf_op jit(solution)/shard_map/ppermute | solution.py:148
  28.1 0.9 %collective-permute-start.10 = (bf16[16,4096]{1,0:T(8,128)(2,1)S(1)}, bf16[16,4096]{1,0:T(8,128)(2,1)S(1)}, u32[]{:S(2)}, u32[]{:S(2)}) collective-permute-start(bf16[16,4096]{1,0:T(8,128)(2,1)S(1)} %collective-permute-done.9.refs_5_), channel_id=1, source_target_pairs={{0,4},{1,5},{2,6},{3,7},{4,0},{5,1},{6,2},{7,3},{8,12},{9,13},{10,... | collective-permute-start | bytes 393224 | tf_op jit(solution)/shard_map/ppermute | solution.py:148
  29.0 2.4 %collective-permute-start.8 = (bf16[16,4096]{1,0:T(8,128)(2,1)S(1)}, bf16[16,4096]{1,0:T(8,128)(2,1)S(1)}, u32[]{:S(2)}, u32[]{:S(2)}) collective-permute-start(bf16[16,4096]{1,0:T(8,128)(2,1)S(1)} %collective-permute-done.3.refs_2_), channel_id=1, source_target_pairs={{0,32},{1,33},{2,34},{3,35},{4,36},{5,37},{6,38},{7,39},{8,40},{9,... | collective-permute-start | bytes 393224 | tf_op jit(solution)/shard_map/ppermute | solution.py:148
  31.5 1.6 %collective-permute-done.10.refs_3_ = bf16[16,4096]{1,0:T(8,128)(2,1)S(1)} collective-permute-done((bf16[16,4096]{1,0:T(8,128)(2,1)S(1)}, bf16[16,4096]{1,0:T(8,128)(2,1)S(1)}, u32[]{:S(2)}, u32[]{:S(2)}) %collective-permute-start.10) | collective-permute-done | bytes 131104 | tf_op jit(solution)/shard_map/ppermute | solution.py:148
  33.1 3.3 %collective-permute-done.8.refs_2_ = bf16[16,4096]{1,0:T(8,128)(2,1)S(1)} collective-permute-done((bf16[16,4096]{1,0:T(8,128)(2,1)S(1)}, bf16[16,4096]{1,0:T(8,128)(2,1)S(1)}, u32[]{:S(2)}, u32[]{:S(2)}) %collective-permute-start.8) | collective-permute-done | bytes 131104 | tf_op jit(solution)/shard_map/ppermute | solution.py:148
  37.0 2.4 %score.1 = f32[256,1024]{1,0:T(8,128)S(1)} custom-call(bf16[256,4096]{1,0:T(8,128)(2,1)S(1)} %bitcast.36, bf16[1024,4096]{1,0:T(8,128)(2,1)S(1)} %bitcast.35), custom_call_target="tpu_custom_call" | custom-call | flops 2147483648 | tf_op jit(solution)/shard_map/score/pallas_call | solution.py:132
  39.5 1.9 %collective-permute-done.14 = f32[2,4,2,8,1024]{4,3,2,1,0:T(8,128)S(1)} collective-permute-done((f32[2,4,2,8,1024]{4,3,2,1,0:T(8,128)S(1)}, f32[2,4,2,8,1024]{4,3,2,1,0:T(8,128)S(1)}, u32[]{:S(2)}, u32[]{:S(2)}) %collective-permute-start.14) | collective-permute-done | bytes 524320 | tf_op jit(solution)/shard_map/ppermute | solution.py:183
  41.4 4.9 %collective-permute-start.15 = (bf16[4,2,8,1024]{3,2,1,0:T(8,128)(2,1)S(1)}, bf16[4,2,8,1024]{3,2,1,0:T(8,128)(2,1)S(1)}, u32[]{:S(2)}, u32[]{:S(2)}) collective-permute-start(bf16[4,2,8,1024]{3,2,1,0:T(8,128)(2,1)S(1)} %fusion.1), channel_id=1, source_target_pairs={{0,128},{64,192},{128,0},{192,64},{1,129},{65,193},{129,1},{193,65... | collective-permute-start | bytes 393224 | tf_op jit(solution)/shard_map/ppermute | solution.py:185
  47.0 6.3 %collective-permute-done.15 = bf16[4,2,8,1024]{3,2,1,0:T(8,128)(2,1)S(1)} collective-permute-done((bf16[4,2,8,1024]{3,2,1,0:T(8,128)(2,1)S(1)}, bf16[4,2,8,1024]{3,2,1,0:T(8,128)(2,1)S(1)}, u32[]{:S(2)}, u32[]{:S(2)}) %collective-permute-start.15) | collective-permute-done | bytes 131104 | tf_op jit(solution)/shard_map/ppermute | solution.py:185
  53.4 0.7 %bitcast_select_fusion = f32[64,1024]{1,0:T(8,128)} fusion(f32[4,2,8,1024]{3,2,1,0:T(8,128)S(1)} %fusion.3, pred[1024]{0:T(1024)(128)(4,1)S(1)} %iota_compare_fusion), kind=kLoop, calls=%fused_computation.10 | loop fusion | flops 65536 | bytes 525312 | tf_op jit(solution)/shard_map/jit(_where)/select_n | solution.py:190
  (29 shorter events, 1.9 us)
Async XLA Ops:
  2.0 6.8 %collective-permute-start = (bf16[4,4096]{1,0:T(4,128)(2,1)S(1)}, bf16[4,4096]{1,0:T(4,128)(2,1)S(1)}, u32[]{:S(2)}, u32[]{:S(2)}) collective-permute-start(bf16[4,4096]{1,0:T(4,128)(2,1)S(1)} %precondition.1), channel_id=1, source_target_pairs={{0,3},{1,2},{2,1},{3,0},{4,7},{5,6},{6,5},{7,4},{8,11},{9,10},{10,... | collective-permute-start | bytes 98312 | tf_op jit(solution)/shard_map/ppermute | solution.py:148
  6.7 4.8 %collective-permute-start.1 = (bf16[4,4096]{1,0:T(4,128)(2,1)S(1)}, bf16[4,4096]{1,0:T(4,128)(2,1)S(1)}, u32[]{:S(2)}, u32[]{:S(2)}) collective-permute-start(bf16[4,4096]{1,0:T(4,128)(2,1)S(1)} %precondition.1), channel_id=1, source_target_pairs={{0,2},{1,3},{2,0},{3,1},{4,6},{5,7},{6,4},{7,5},{8,10},{9,11},{10,... | collective-permute-start | bytes 98312 | tf_op jit(solution)/shard_map/ppermute | solution.py:148
  6.7 4.8 %collective-permute-start.2 = (bf16[4,4096]{1,0:T(4,128)(2,1)S(1)}, bf16[4,4096]{1,0:T(4,128)(2,1)S(1)}, u32[]{:S(2)}, u32[]{:S(2)}) collective-permute-start(bf16[4,4096]{1,0:T(4,128)(2,1)S(1)} %precondition.1), channel_id=1, source_target_pairs={{0,1},{1,0},{2,3},{3,2},{4,5},{5,4},{6,7},{7,6},{8,9},{9,8},{10,11... | collective-permute-start | bytes 98312 | tf_op jit(solution)/shard_map/ppermute | solution.py:148
  11.7 8.3 %collective-permute-start.5 = (bf16[16,4096]{1,0:T(8,128)(2,1)S(1)}, bf16[16,4096]{1,0:T(8,128)(2,1)S(1)}, u32[]{:S(2)}, u32[]{:S(2)}) collective-permute-start(bf16[16,4096]{1,0:T(8,128)(2,1)S(1)} %pad_maximum_fusion.2.refs_0_), channel_id=1, source_target_pairs={{0,12},{1,13},{2,14},{3,15},{4,8},{5,9},{6,10},{7,11},{8,4},{9,5},... | collective-permute-start | bytes 393224 | tf_op jit(solution)/shard_map/ppermute | solution.py:148
  12.3 10.9 %collective-permute-start.3 = (bf16[16,4096]{1,0:T(8,128)(2,1)S(1)}, bf16[16,4096]{1,0:T(8,128)(2,1)S(1)}, u32[]{:S(2)}, u32[]{:S(2)}) collective-permute-start(bf16[16,4096]{1,0:T(8,128)(2,1)S(1)} %pad_maximum_fusion.2.refs_0_), channel_id=1, source_target_pairs={{0,8},{1,9},{2,10},{3,11},{4,12},{5,13},{6,14},{7,15},{8,0},{9,1},... | collective-permute-start | bytes 393224 | tf_op jit(solution)/shard_map/ppermute | solution.py:148
  14.7 8.5 %collective-permute-start.4 = (bf16[16,4096]{1,0:T(8,128)(2,1)S(1)}, bf16[16,4096]{1,0:T(8,128)(2,1)S(1)}, u32[]{:S(2)}, u32[]{:S(2)}) collective-permute-start(bf16[16,4096]{1,0:T(8,128)(2,1)S(1)} %pad_maximum_fusion.2.refs_0_), channel_id=1, source_target_pairs={{0,4},{1,5},{2,6},{3,7},{4,0},{5,1},{6,2},{7,3},{8,12},{9,13},{10,... | collective-permute-start | bytes 393224 | tf_op jit(solution)/shard_map/ppermute | solution.py:148
  15.9 8.6 %collective-permute-start.11 = (bf16[16,4096]{1,0:T(8,128)(2,1)S(1)}, bf16[16,4096]{1,0:T(8,128)(2,1)S(1)}, u32[]{:S(2)}, u32[]{:S(2)}) collective-permute-start(bf16[16,4096]{1,0:T(8,128)(2,1)S(1)} %pad_maximum_fusion.2.refs_0_), channel_id=1, source_target_pairs={{0,16},{1,17},{2,18},{3,19},{4,20},{5,21},{6,22},{7,23},{8,24},{9,... | collective-permute-start | bytes 393224 | tf_op jit(solution)/shard_map/ppermute | solution.py:148
  17.5 7.6 %collective-permute-start.12 = (bf16[16,4096]{1,0:T(8,128)(2,1)S(1)}, bf16[16,4096]{1,0:T(8,128)(2,1)S(1)}, u32[]{:S(2)}, u32[]{:S(2)}) collective-permute-start(bf16[16,4096]{1,0:T(8,128)(2,1)S(1)} %pad_maximum_fusion.2.refs_0_), channel_id=1, source_target_pairs={{0,48},{1,49},{2,50},{3,51},{4,52},{5,53},{6,54},{7,55},{8,56},{9,... | collective-permute-start | bytes 393224 | tf_op jit(solution)/shard_map/ppermute | solution.py:148
  20.0 7.5 %collective-permute-start.9 = (bf16[16,4096]{1,0:T(8,128)(2,1)S(1)}, bf16[16,4096]{1,0:T(8,128)(2,1)S(1)}, u32[]{:S(2)}, u32[]{:S(2)}) collective-permute-start(bf16[16,4096]{1,0:T(8,128)(2,1)S(1)} %pad_maximum_fusion.2.refs_0_), channel_id=1, source_target_pairs={{0,32},{1,33},{2,34},{3,35},{4,36},{5,37},{6,38},{7,39},{8,40},{9,... | collective-permute-start | bytes 393224 | tf_op jit(solution)/shard_map/ppermute | solution.py:148
  23.2 13.2 %collective-permute-start.6 = (bf16[40,4096]{1,0:T(8,128)(2,1)S(1)}, bf16[40,4096]{1,0:T(8,128)(2,1)S(1)}, u32[]{:S(2)}, u32[]{:S(2)}) collective-permute-start(bf16[40,4096]{1,0:T(8,128)(2,1)S(1)} %pad_maximum_fusion), channel_id=1, source_target_pairs={{0,16},{1,17},{2,18},{3,19},{4,20},{5,21},{6,22},{7,23},{8,24},{9,... | collective-permute-start | bytes 983048 | tf_op jit(solution)/shard_map/ppermute | solution.py:148
  24.0 12.8 %collective-permute-start.7 = (bf16[40,4096]{1,0:T(8,128)(2,1)S(1)}, bf16[40,4096]{1,0:T(8,128)(2,1)S(1)}, u32[]{:S(2)}, u32[]{:S(2)}) collective-permute-start(bf16[40,4096]{1,0:T(8,128)(2,1)S(1)} %pad_maximum_fusion), channel_id=1, source_target_pairs={{0,48},{1,49},{2,50},{3,51},{4,52},{5,53},{6,54},{7,55},{8,56},{9,... | collective-permute-start | bytes 983048 | tf_op jit(solution)/shard_map/ppermute | solution.py:148
  27.5 9.5 %slice-start = ((s8[8388608]{0:T(1024)(128)(4,1)}), s8[4194304]{0:T(1024)(128)(4,1)S(1)}, s32[]{:S(2)}) async-start(s8[8388608]{0:T(1024)(128)(4,1)} %bitcast.33), calls=%async_computation | async-start | bytes 8388608
  27.5 9.5 %slice-start.1 = ((s8[8388608]{0:T(1024)(128)(4,1)}), s8[4194304]{0:T(1024)(128)(4,1)S(1)}, s32[]{:S(2)}) async-start(s8[8388608]{0:T(1024)(128)(4,1)} %bitcast.33), calls=%async_computation.1 | async-start | bytes 8388608
  27.5 8.9 %collective-permute-start.13 = (bf16[32,4096]{1,0:T(8,128)(2,1)S(1)}, bf16[32,4096]{1,0:T(8,128)(2,1)S(1)}, u32[]{:S(2)}, u32[]{:S(2)}) collective-permute-start(bf16[32,4096]{1,0:T(8,128)(2,1)S(1)} %pad_maximum_fusion.1), channel_id=1, source_target_pairs={{0,12},{1,13},{2,14},{3,15},{4,8},{5,9},{6,10},{7,11},{8,4},{9,5},... | collective-permute-start | bytes 786440 | tf_op jit(solution)/shard_map/ppermute | solution.py:148
  28.1 5.0 %collective-permute-start.10 = (bf16[16,4096]{1,0:T(8,128)(2,1)S(1)}, bf16[16,4096]{1,0:T(8,128)(2,1)S(1)}, u32[]{:S(2)}, u32[]{:S(2)}) collective-permute-start(bf16[16,4096]{1,0:T(8,128)(2,1)S(1)} %collective-permute-done.9.refs_5_), channel_id=1, source_target_pairs={{0,4},{1,5},{2,6},{3,7},{4,0},{5,1},{6,2},{7,3},{8,12},{9,13},{10,... | collective-permute-start | bytes 393224 | tf_op jit(solution)/shard_map/ppermute | solution.py:148
  29.0 7.4 %collective-permute-start.8 = (bf16[16,4096]{1,0:T(8,128)(2,1)S(1)}, bf16[16,4096]{1,0:T(8,128)(2,1)S(1)}, u32[]{:S(2)}, u32[]{:S(2)}) collective-permute-start(bf16[16,4096]{1,0:T(8,128)(2,1)S(1)} %collective-permute-done.3.refs_2_), channel_id=1, source_target_pairs={{0,32},{1,33},{2,34},{3,35},{4,36},{5,37},{6,38},{7,39},{8,40},{9,... | collective-permute-start | bytes 393224 | tf_op jit(solution)/shard_map/ppermute | solution.py:148
  39.4 2.0 %collective-permute-start.14 = (f32[2,4,2,8,1024]{4,3,2,1,0:T(8,128)S(1)}, f32[2,4,2,8,1024]{4,3,2,1,0:T(8,128)S(1)}, u32[]{:S(2)}, u32[]{:S(2)}) collective-permute-start(f32[2,4,2,8,1024]{4,3,2,1,0:T(8,128)S(1)} %bitcast.39), channel_id=1, source_target_pairs={{0,64},{64,0},{128,192},{192,128},{1,65},{65,1},{129,193},{193,129... | collective-permute-start | bytes 1572872 | tf_op jit(solution)/shard_map/ppermute | solution.py:183
  41.4 11.9 %collective-permute-start.15 = (bf16[4,2,8,1024]{3,2,1,0:T(8,128)(2,1)S(1)}, bf16[4,2,8,1024]{3,2,1,0:T(8,128)(2,1)S(1)}, u32[]{:S(2)}, u32[]{:S(2)}) collective-permute-start(bf16[4,2,8,1024]{3,2,1,0:T(8,128)(2,1)S(1)} %fusion.1), channel_id=1, source_target_pairs={{0,128},{64,192},{128,0},{192,64},{1,129},{65,193},{129,1},{193,65... | collective-permute-start | bytes 393224 | tf_op jit(solution)/shard_map/ppermute | solution.py:185
